TPU v7x, 512 devices: a whole 4x4x16 slice. The times are simulated.
512 devices in a mesh: stream: 16 (over x, y), cross: 32 (over z, core).
Axes of the slice: x: 4, y: 4, z: 16, core: 2. Of those that a mesh axis runs over, the one named last changes fastest.
Arguments:
- inflow: float32 [2, 8, 5, 256, 256], P(None, None, None, 'cross'), may hold values from -6 to 6
- source_shape: float32 [5, 256, 256], P(None, 'cross'), may hold values from -6 to 6
- source_amp: float32 [16, 2, 8], P('stream'), may hold values from -3 to 3
- coupling: float32 [4, 4, 5, 5], replicated, may hold values from -0.4375 to 0.4375
- omega: float32 [8], replicated, may hold values from 0.05 to 0.25
- rec_coef: float32 [4], replicated, may hold values from 0.7 to 1
- rec_order: int32 [4], replicated, may hold values from 0 to 3, each once
- station_zone: int32 [16], P('stream'), may hold values from 0 to 3
- solid_mask: int32 [256, 256], P('cross'), may hold values from 0 to 1, as said below
Outputs:
- group_exits: float32 [16, 2, 8, 5, 256, 256], P('stream', None, None, None, 'cross')
Inputs may be any that keep to these rules, and one draw needn't show every extreme that they name: rec_order holds each of 0 .. 3 once. `solid_mask`: 1 marks a solid cell, 0 a fluid cell.
All inputs are finite; a program needn't handle non-finite values.
Results may differ from a plain program's by a relative error of at most 0.00011.
Values sent between devices are 32-bit elements; how exact they have to be, the bound alone decides.
A program may use at most 64 MiB of HBM per device.

v0:
```python
import math

import jax
import jax.numpy as jnp
from jax import lax
from jax.sharding import PartitionSpec as P

viscosity = 0.05
penalty = 0.5
damping = 0.03


def with_halo(x, sides, width):
    for axis, dim in sides:
        size, length = (lax.axis_size(axis), x.shape[dim])
        up = [(i, (i + 1) % size) for i in range(size - 1)]
        down = [(j, i) for i, j in up]
        last = lax.slice_in_dim(x, length - width, length, axis=dim)
        first = lax.slice_in_dim(x, 0, width, axis=dim)
        before = lax.ppermute(last, axis, up)
        after = lax.ppermute(first, axis, down)
        x = jnp.concatenate([before, x, after], axis=dim)
    return x


def in_one_piece(arrays, axis, dim, along):
    widths = [math.prod(a.shape[along:]) for a in arrays]
    both = jnp.concatenate(
        [a.reshape(*a.shape[:along], w) for a, w in zip(arrays, widths)], axis=along
    )
    out = lax.all_gather(both, axis, axis=dim, tiled=True)
    pieces = jnp.split(out, [sum(widths[:k]) for k in range(1, len(widths))], axis=along)
    return tuple((b.reshape(*out.shape[:along], *a.shape[along:]) for a, b in zip(arrays, pieces)))


def station_operators(matrices):
    var_count = matrices.shape[-1]
    advect_rows = 0.5 * (matrices[0] + matrices[0].T)
    advect_cols = 0.5 * (matrices[1] + matrices[1].T)
    rotation_part = 0.5 * (matrices[2] - matrices[2].T)
    viscous = viscosity * (
        jnp.eye(var_count, dtype=jnp.float32)
        + jnp.dot(matrices[3], matrices[3].T, precision=lax.Precision.HIGHEST)
    )
    return jnp.stack([advect_rows, advect_cols, rotation_part, viscous])


def apply_operator(padded, operators, damp_field, frequency):
    center = padded[:, :, :, 1:-1, :]
    row_next = padded[:, :, :, 2:, :]
    row_prev = padded[:, :, :, :-2, :]
    col_next = jnp.roll(center, -1, axis=4)
    col_prev = jnp.roll(center, 1, axis=4)
    stencil = jnp.stack(
        [
            0.5 * (row_next - row_prev),
            0.5 * (col_next - col_prev),
            center,
            row_next + row_prev + col_next + col_prev - 4.0 * center,
        ]
    )
    coupled = jnp.einsum("kvw,krfwyz->rfvyz", operators, stencil, precision=lax.Precision.HIGHEST)
    spinning = frequency[:, None, None, None]
    turning = jnp.stack([spinning * center[1], -spinning * center[0]])
    return coupled - damp_field * center + turning


def level_factors(rec_coef, rec_order):
    levels = rec_coef.shape[0]
    picked = jnp.sum(
        jnp.where(
            rec_order[:, None] == jnp.arange(levels, dtype=jnp.int32)[None, :],
            rec_coef[None, :],
            jnp.zeros((), jnp.float32),
        ),
        axis=1,
    )
    return picked / (levels - jnp.arange(levels, dtype=jnp.int32)).astype(jnp.float32)


def on_device(
    inflow, source_shape, source_amp, coupling, omega, rec_coef, rec_order, station_zone, solid_mask
):
    stream_count = lax.axis_size("stream")
    stream_pos = lax.axis_index("stream")
    cross_count = lax.axis_size("cross")
    cross_pos = lax.axis_index("cross")
    row_count = solid_mask.shape[0]
    levels = rec_coef.shape[0]
    freq_count = omega.shape[0]
    station_count = station_zone.shape[0]
    damp_field = penalty * solid_mask.astype(jnp.float32) + damping
    factors = level_factors(rec_coef, rec_order)
    one_hot = (
        station_zone[:, None] == jnp.arange(coupling.shape[0], dtype=jnp.int32)[None, :]
    ).astype(jnp.float32)
    selected = jnp.einsum("sz,zkvw->skvw", one_hot, coupling, precision=lax.Precision.HIGHEST)
    operators_all = jax.vmap(station_operators)(selected)
    damp_deep = with_halo(damp_field, (("cross", 0),), levels)
    global_rows = (
        cross_pos * row_count - levels + jnp.arange(row_count + 2 * levels, dtype=jnp.int32)
    )
    inside = ((global_rows >= 0) & (global_rows < row_count * cross_count)).astype(jnp.float32)

    def recursion(marched, operators, frequency):
        extended = with_halo(marched, (("cross", 3),), levels)
        current = extended
        for depth_step in range(levels):
            row_start = depth_step + 1
            row_stop = row_start + row_count + 2 * (levels - depth_step - 1)
            refreshed = extended[:, :, :, row_start:row_stop, :] + factors[
                depth_step
            ] * apply_operator(current, operators, damp_deep[row_start:row_stop], frequency)
            current = refreshed * inside[row_start:row_stop][:, None]
        return current

    freq_groups = min(stream_count, freq_count)
    freq_width = freq_count // freq_groups
    freq_start = stream_pos % freq_groups * freq_width
    operators_every, amps_every = in_one_piece((operators_all, source_amp), "stream", 0, 1)
    own_frequency = lax.dynamic_slice_in_dim(omega, freq_start, freq_width)
    own_amplitudes = lax.dynamic_slice_in_dim(amps_every, freq_start, freq_width, axis=2)
    own_inflow = lax.dynamic_slice_in_dim(inflow, freq_start, freq_width, axis=1)

    def group_march(marched, group_index):

        def local_station(offset, carried):
            station = group_index * station_count + offset
            station_ops = lax.dynamic_index_in_dim(operators_every, station, keepdims=False)
            weights = lax.dynamic_index_in_dim(own_amplitudes, station, keepdims=False)
            return (
                recursion(carried, station_ops, own_frequency)
                + weights[:, :, None, None, None] * source_shape[None, None]
            )

        advanced = lax.fori_loop(0, station_count, local_station, marched)
        return (advanced, advanced)

    final_state, exits = lax.scan(
        group_march, own_inflow, jnp.arange(stream_count, dtype=jnp.int32)
    )
    placed = lax.all_to_all(exits, "stream", split_axis=0, concat_axis=2, tiled=True)
    return placed[:, :, :freq_count]


def solution(mesh):
    placed = (
        P(None, None, None, "cross", None),
        P(None, "cross", None),
        P("stream", None, None),
        P(),
        P(),
        P(),
        P(),
        P("stream"),
        P("cross", None),
    )
    return jax.shard_map(
        on_device,
        mesh=mesh,
        in_specs=placed,
        out_specs=P("stream", None, None, None, "cross", None),
        check_vma=False,
    )
```

profile of v0, /device:TPU:97, one launch (start us, length us, event | category | flops | bytes accessed | tf_op | source)
XLA Modules:
  0.0 442.2 jit_solution(8979155962303686298)
XLA Ops:
  0.8 5.3 %collective-permute-start.2 = (f32[4,256]{1,0:T(4,128)S(1)}, f32[4,256]{1,0:T(4,128)S(1)}, u32[]{:S(2)}, u32[]{:S(2)}) collective-permute-start(f32[4,256]{1,0:T(4,128)S(1)} %get-tuple-element.292), channel_id=1, source_target_pairs={{0,1},{1,2},{2,3},{3,4},{4,5},{5,6},{6,7},{7,8},{8,9},{9,10},{10,1... | collective-permute-start | bytes 12296 | tf_op jit(solution)/shard_map/ppermute | solution.py:20
  6.1 1.9 collective-permute-start.3
  11.1 16.3 %all-gather = f32[16,1,116]{2,1,0:T(1,128)S(1)} all-gather(f32[1,1,116]{2,1,0:T(1,128)S(1)} %maximum_bitcast_fusion.15), channel_id=1, replica_groups=mesh['stream'=16,'cross'=32] {'stream'}, dimensions={0}, use_global_device_ids=true | all-gather | bytes 7888 | tf_op jit(solution)/shard_map/all_gather | solution.py:31
  31.6 386.3 %while.13 = (s32[]{:T(128)}, f32[2,1,5,8,256]{4,2,3,0,1:T(8,128)S(1)}, f32[16,2,1,5,8,256]{5,4,3,1,2,0:T(8,128)}, f32[4]{0:T(128)S(1)}, s32[16]{0:T(128)S(1)}, /...) while((s32[]{:T(128)}, ...), condition=%wide.region_2.3_spmd, body=%wide.region_1.2_spmd.sunk | while | flops 30791684 | bytes 13964863 | solution.py:139
  31.7 9.5 %collective-permute-start = (f32[2,1,5,4,256]{4,2,3,0,1:T(8,128)S(1)}, f32[2,1,5,4,256]{4,2,3,0,1:T(8,128)S(1)}, u32[]{:S(2)}, u32[]{:S(2)}) collective-permute-start(f32[2,1,5,4,256]{4,2,3,0,1:T(8,128)S(1)} %get-tuple-element.423), channel_id=1, source_target_pairs={{0,1},{1,2},{2,3},{3,4},{4,5},{5,6},{6,7},{7,8},{8,9},{9,10},{10,1... | collective-permute-start | bytes 122888 | tf_op jit(solution)/shard_map/while/body/eval_jaxpr/while/body/eval_jaxpr/ppermute | solution.py:20
  41.2 1.9 collective-permute-start.1
  61.3 3.6 collective-permute-start
  64.9 1.9 collective-permute-start.1
  73.7 1.4 fusion.107
  85.1 3.6 collective-permute-start
  88.7 1.9 collective-permute-start.1
  97.5 1.4 fusion.107
  108.9 3.6 collective-permute-start
  112.5 1.9 collective-permute-start.1
  121.3 1.4 fusion.107
  132.6 3.6 collective-permute-start
  136.2 1.9 collective-permute-start.1
  145.0 1.4 fusion.107
  156.4 3.6 collective-permute-start
  160.0 1.9 collective-permute-start.1
  180.2 3.6 collective-permute-start
  183.8 1.9 collective-permute-start.1
  192.6 1.4 fusion.107
  204.0 3.6 collective-permute-start
  207.6 1.9 collective-permute-start.1
  216.4 1.4 fusion.107
  227.8 3.6 collective-permute-start
  231.4 1.9 collective-permute-start.1
  240.1 1.4 fusion.107
  251.5 3.6 collective-permute-start
  255.1 1.9 collective-permute-start.1
  275.3 3.6 collective-permute-start
  278.9 1.9 collective-permute-start.1
  287.7 1.4 fusion.107
  299.1 3.6 collective-permute-start
  302.7 1.9 collective-permute-start.1
  311.5 1.4 fusion.107
  322.9 3.6 collective-permute-start
  326.5 1.9 collective-permute-start.1
  335.3 1.4 fusion.107
  346.7 3.6 collective-permute-start
  350.3 1.9 collective-permute-start.1
  359.0 1.4 fusion.107
  370.4 3.6 collective-permute-start
  374.0 1.9 collective-permute-start.1
  394.2 3.6 collective-permute-start
  397.8 1.9 collective-permute-start.1
  418.0 23.3 %all_to_all.18 = f32[16,2,1,5,8,256]{5,4,3,1,2,0:T(8,128)S(1)} all-to-all(f32[16,2,1,5,8,256]{5,4,3,1,2,0:T(8,128)} %get-tuple-element.156), channel_id=1, replica_groups=mesh['stream'=16,'cross'=32] {'stream'}, dimensions={0} | all-to-all | bytes 2621440 | tf_op jit(solution)/shard_map/all_to_all | solution.py:142
  (1003 shorter events, 249.7 us)
Async XLA Ops:
  0.0 27.5 %copy-start = (f32[2,8,5,8,256]{4,3,2,1,0:T(8,128)S(1)}, f32[2,8,5,8,256]{4,3,2,1,0:T(8,128)}, u32[]{:S(2)}) copy-start(f32[2,8,5,8,256]{4,3,2,1,0:T(8,128)} %param.11) | copy-start | bytes 1966084
  0.8 30.8 %collective-permute-start.2 = (f32[4,256]{1,0:T(4,128)S(1)}, f32[4,256]{1,0:T(4,128)S(1)}, u32[]{:S(2)}, u32[]{:S(2)}) collective-permute-start(f32[4,256]{1,0:T(4,128)S(1)} %get-tuple-element.292), channel_id=1, source_target_pairs={{0,1},{1,2},{2,3},{3,4},{4,5},{5,6},{6,7},{7,8},{8,9},{9,10},{10,1... | collective-permute-start | bytes 12296 | tf_op jit(solution)/shard_map/ppermute | solution.py:20
  6.1 25.5 %collective-permute-start.3 = (f32[4,256]{1,0:T(4,128)S(1)}, f32[4,256]{1,0:T(4,128)S(1)}, u32[]{:S(2)}, u32[]{:S(2)}) collective-permute-start(f32[4,256]{1,0:T(4,128)S(1)} %get-tuple-element.293), channel_id=1, source_target_pairs={{1,0},{2,1},{3,2},{4,3},{5,4},{6,5},{7,6},{8,7},{9,8},{10,9},{11,1... | collective-permute-start | bytes 12296 | tf_op jit(solution)/shard_map/ppermute | solution.py:21
  31.7 15.0 %collective-permute-start = (f32[2,1,5,4,256]{4,2,3,0,1:T(8,128)S(1)}, f32[2,1,5,4,256]{4,2,3,0,1:T(8,128)S(1)}, u32[]{:S(2)}, u32[]{:S(2)}) collective-permute-start(f32[2,1,5,4,256]{4,2,3,0,1:T(8,128)S(1)} %get-tuple-element.423), channel_id=1, source_target_pairs={{0,1},{1,2},{2,3},{3,4},{4,5},{5,6},{6,7},{7,8},{8,9},{9,10},{10,1... | collective-permute-start | bytes 122888 | tf_op jit(solution)/shard_map/while/body/eval_jaxpr/while/body/eval_jaxpr/ppermute | solution.py:20
  41.2 6.8 %collective-permute-start.1 = (f32[2,1,5,4,256]{4,2,3,0,1:T(8,128)S(1)}, f32[2,1,5,4,256]{4,2,3,0,1:T(8,128)S(1)}, u32[]{:S(2)}, u32[]{:S(2)}) collective-permute-start(f32[2,1,5,4,256]{4,2,3,0,1:T(8,128)S(1)} %get-tuple-element.424), channel_id=1, source_target_pairs={{1,0},{2,1},{3,2},{4,3},{5,4},{6,5},{7,6},{8,7},{9,8},{10,9},{11,1... | collective-permute-start | bytes 122888 | tf_op jit(solution)/shard_map/while/body/eval_jaxpr/while/body/eval_jaxpr/ppermute | solution.py:21
  61.3 9.1 %collective-permute-start = (f32[2,1,5,4,256]{4,2,3,0,1:T(8,128)S(1)}, f32[2,1,5,4,256]{4,2,3,0,1:T(8,128)S(1)}, u32[]{:S(2)}, u32[]{:S(2)}) collective-permute-start(f32[2,1,5,4,256]{4,2,3,0,1:T(8,128)S(1)} %get-tuple-element.423), channel_id=1, source_target_pairs={{0,1},{1,2},{2,3},{3,4},{4,5},{5,6},{6,7},{7,8},{8,9},{9,10},{10,1... | collective-permute-start | bytes 122888 | tf_op jit(solution)/shard_map/while/body/eval_jaxpr/while/body/eval_jaxpr/ppermute | solution.py:20
  64.9 6.8 %collective-permute-start.1 = (f32[2,1,5,4,256]{4,2,3,0,1:T(8,128)S(1)}, f32[2,1,5,4,256]{4,2,3,0,1:T(8,128)S(1)}, u32[]{:S(2)}, u32[]{:S(2)}) collective-permute-start(f32[2,1,5,4,256]{4,2,3,0,1:T(8,128)S(1)} %get-tuple-element.424), channel_id=1, source_target_pairs={{1,0},{2,1},{3,2},{4,3},{5,4},{6,5},{7,6},{8,7},{9,8},{10,9},{11,1... | collective-permute-start | bytes 122888 | tf_op jit(solution)/shard_map/while/body/eval_jaxpr/while/body/eval_jaxpr/ppermute | solution.py:21
  85.1 9.1 %collective-permute-start = (f32[2,1,5,4,256]{4,2,3,0,1:T(8,128)S(1)}, f32[2,1,5,4,256]{4,2,3,0,1:T(8,128)S(1)}, u32[]{:S(2)}, u32[]{:S(2)}) collective-permute-start(f32[2,1,5,4,256]{4,2,3,0,1:T(8,128)S(1)} %get-tuple-element.423), channel_id=1, source_target_pairs={{0,1},{1,2},{2,3},{3,4},{4,5},{5,6},{6,7},{7,8},{8,9},{9,10},{10,1... | collective-permute-start | bytes 122888 | tf_op jit(solution)/shard_map/while/body/eval_jaxpr/while/body/eval_jaxpr/ppermute | solution.py:20
  88.7 6.8 %collective-permute-start.1 = (f32[2,1,5,4,256]{4,2,3,0,1:T(8,128)S(1)}, f32[2,1,5,4,256]{4,2,3,0,1:T(8,128)S(1)}, u32[]{:S(2)}, u32[]{:S(2)}) collective-permute-start(f32[2,1,5,4,256]{4,2,3,0,1:T(8,128)S(1)} %get-tuple-element.424), channel_id=1, source_target_pairs={{1,0},{2,1},{3,2},{4,3},{5,4},{6,5},{7,6},{8,7},{9,8},{10,9},{11,1... | collective-permute-start | bytes 122888 | tf_op jit(solution)/shard_map/while/body/eval_jaxpr/while/body/eval_jaxpr/ppermute | solution.py:21
  108.9 9.1 %collective-permute-start = (f32[2,1,5,4,256]{4,2,3,0,1:T(8,128)S(1)}, f32[2,1,5,4,256]{4,2,3,0,1:T(8,128)S(1)}, u32[]{:S(2)}, u32[]{:S(2)}) collective-permute-start(f32[2,1,5,4,256]{4,2,3,0,1:T(8,128)S(1)} %get-tuple-element.423), channel_id=1, source_target_pairs={{0,1},{1,2},{2,3},{3,4},{4,5},{5,6},{6,7},{7,8},{8,9},{9,10},{10,1... | collective-permute-start | bytes 122888 | tf_op jit(solution)/shard_map/while/body/eval_jaxpr/while/body/eval_jaxpr/ppermute | solution.py:20
  112.5 6.8 %collective-permute-start.1 = (f32[2,1,5,4,256]{4,2,3,0,1:T(8,128)S(1)}, f32[2,1,5,4,256]{4,2,3,0,1:T(8,128)S(1)}, u32[]{:S(2)}, u32[]{:S(2)}) collective-permute-start(f32[2,1,5,4,256]{4,2,3,0,1:T(8,128)S(1)} %get-tuple-element.424), channel_id=1, source_target_pairs={{1,0},{2,1},{3,2},{4,3},{5,4},{6,5},{7,6},{8,7},{9,8},{10,9},{11,1... | collective-permute-start | bytes 122888 | tf_op jit(solution)/shard_map/while/body/eval_jaxpr/while/body/eval_jaxpr/ppermute | solution.py:21
  132.6 9.1 %collective-permute-start = (f32[2,1,5,4,256]{4,2,3,0,1:T(8,128)S(1)}, f32[2,1,5,4,256]{4,2,3,0,1:T(8,128)S(1)}, u32[]{:S(2)}, u32[]{:S(2)}) collective-permute-start(f32[2,1,5,4,256]{4,2,3,0,1:T(8,128)S(1)} %get-tuple-element.423), channel_id=1, source_target_pairs={{0,1},{1,2},{2,3},{3,4},{4,5},{5,6},{6,7},{7,8},{8,9},{9,10},{10,1... | collective-permute-start | bytes 122888 | tf_op jit(solution)/shard_map/while/body/eval_jaxpr/while/body/eval_jaxpr/ppermute | solution.py:20
  136.2 6.8 %collective-permute-start.1 = (f32[2,1,5,4,256]{4,2,3,0,1:T(8,128)S(1)}, f32[2,1,5,4,256]{4,2,3,0,1:T(8,128)S(1)}, u32[]{:S(2)}, u32[]{:S(2)}) collective-permute-start(f32[2,1,5,4,256]{4,2,3,0,1:T(8,128)S(1)} %get-tuple-element.424), channel_id=1, source_target_pairs={{1,0},{2,1},{3,2},{4,3},{5,4},{6,5},{7,6},{8,7},{9,8},{10,9},{11,1... | collective-permute-start | bytes 122888 | tf_op jit(solution)/shard_map/while/body/eval_jaxpr/while/body/eval_jaxpr/ppermute | solution.py:21
  156.4 9.1 %collective-permute-start = (f32[2,1,5,4,256]{4,2,3,0,1:T(8,128)S(1)}, f32[2,1,5,4,256]{4,2,3,0,1:T(8,128)S(1)}, u32[]{:S(2)}, u32[]{:S(2)}) collective-permute-start(f32[2,1,5,4,256]{4,2,3,0,1:T(8,128)S(1)} %get-tuple-element.423), channel_id=1, source_target_pairs={{0,1},{1,2},{2,3},{3,4},{4,5},{5,6},{6,7},{7,8},{8,9},{9,10},{10,1... | collective-permute-start | bytes 122888 | tf_op jit(solution)/shard_map/while/body/eval_jaxpr/while/body/eval_jaxpr/ppermute | solution.py:20
  160.0 6.8 %collective-permute-start.1 = (f32[2,1,5,4,256]{4,2,3,0,1:T(8,128)S(1)}, f32[2,1,5,4,256]{4,2,3,0,1:T(8,128)S(1)}, u32[]{:S(2)}, u32[]{:S(2)}) collective-permute-start(f32[2,1,5,4,256]{4,2,3,0,1:T(8,128)S(1)} %get-tuple-element.424), channel_id=1, source_target_pairs={{1,0},{2,1},{3,2},{4,3},{5,4},{6,5},{7,6},{8,7},{9,8},{10,9},{11,1... | collective-permute-start | bytes 122888 | tf_op jit(solution)/shard_map/while/body/eval_jaxpr/while/body/eval_jaxpr/ppermute | solution.py:21
  180.2 9.1 %collective-permute-start = (f32[2,1,5,4,256]{4,2,3,0,1:T(8,128)S(1)}, f32[2,1,5,4,256]{4,2,3,0,1:T(8,128)S(1)}, u32[]{:S(2)}, u32[]{:S(2)}) collective-permute-start(f32[2,1,5,4,256]{4,2,3,0,1:T(8,128)S(1)} %get-tuple-element.423), channel_id=1, source_target_pairs={{0,1},{1,2},{2,3},{3,4},{4,5},{5,6},{6,7},{7,8},{8,9},{9,10},{10,1... | collective-permute-start | bytes 122888 | tf_op jit(solution)/shard_map/while/body/eval_jaxpr/while/body/eval_jaxpr/ppermute | solution.py:20
  183.8 6.8 %collective-permute-start.1 = (f32[2,1,5,4,256]{4,2,3,0,1:T(8,128)S(1)}, f32[2,1,5,4,256]{4,2,3,0,1:T(8,128)S(1)}, u32[]{:S(2)}, u32[]{:S(2)}) collective-permute-start(f32[2,1,5,4,256]{4,2,3,0,1:T(8,128)S(1)} %get-tuple-element.424), channel_id=1, source_target_pairs={{1,0},{2,1},{3,2},{4,3},{5,4},{6,5},{7,6},{8,7},{9,8},{10,9},{11,1... | collective-permute-start | bytes 122888 | tf_op jit(solution)/shard_map/while/body/eval_jaxpr/while/body/eval_jaxpr/ppermute | solution.py:21
  204.0 9.1 %collective-permute-start = (f32[2,1,5,4,256]{4,2,3,0,1:T(8,128)S(1)}, f32[2,1,5,4,256]{4,2,3,0,1:T(8,128)S(1)}, u32[]{:S(2)}, u32[]{:S(2)}) collective-permute-start(f32[2,1,5,4,256]{4,2,3,0,1:T(8,128)S(1)} %get-tuple-element.423), channel_id=1, source_target_pairs={{0,1},{1,2},{2,3},{3,4},{4,5},{5,6},{6,7},{7,8},{8,9},{9,10},{10,1... | collective-permute-start | bytes 122888 | tf_op jit(solution)/shard_map/while/body/eval_jaxpr/while/body/eval_jaxpr/ppermute | solution.py:20
  207.6 6.8 %collective-permute-start.1 = (f32[2,1,5,4,256]{4,2,3,0,1:T(8,128)S(1)}, f32[2,1,5,4,256]{4,2,3,0,1:T(8,128)S(1)}, u32[]{:S(2)}, u32[]{:S(2)}) collective-permute-start(f32[2,1,5,4,256]{4,2,3,0,1:T(8,128)S(1)} %get-tuple-element.424), channel_id=1, source_target_pairs={{1,0},{2,1},{3,2},{4,3},{5,4},{6,5},{7,6},{8,7},{9,8},{10,9},{11,1... | collective-permute-start | bytes 122888 | tf_op jit(solution)/shard_map/while/body/eval_jaxpr/while/body/eval_jaxpr/ppermute | solution.py:21
  227.8 9.1 %collective-permute-start = (f32[2,1,5,4,256]{4,2,3,0,1:T(8,128)S(1)}, f32[2,1,5,4,256]{4,2,3,0,1:T(8,128)S(1)}, u32[]{:S(2)}, u32[]{:S(2)}) collective-permute-start(f32[2,1,5,4,256]{4,2,3,0,1:T(8,128)S(1)} %get-tuple-element.423), channel_id=1, source_target_pairs={{0,1},{1,2},{2,3},{3,4},{4,5},{5,6},{6,7},{7,8},{8,9},{9,10},{10,1... | collective-permute-start | bytes 122888 | tf_op jit(solution)/shard_map/while/body/eval_jaxpr/while/body/eval_jaxpr/ppermute | solution.py:20
  231.4 6.8 %collective-permute-start.1 = (f32[2,1,5,4,256]{4,2,3,0,1:T(8,128)S(1)}, f32[2,1,5,4,256]{4,2,3,0,1:T(8,128)S(1)}, u32[]{:S(2)}, u32[]{:S(2)}) collective-permute-start(f32[2,1,5,4,256]{4,2,3,0,1:T(8,128)S(1)} %get-tuple-element.424), channel_id=1, source_target_pairs={{1,0},{2,1},{3,2},{4,3},{5,4},{6,5},{7,6},{8,7},{9,8},{10,9},{11,1... | collective-permute-start | bytes 122888 | tf_op jit(solution)/shard_map/while/body/eval_jaxpr/while/body/eval_jaxpr/ppermute | solution.py:21
  251.5 9.1 %collective-permute-start = (f32[2,1,5,4,256]{4,2,3,0,1:T(8,128)S(1)}, f32[2,1,5,4,256]{4,2,3,0,1:T(8,128)S(1)}, u32[]{:S(2)}, u32[]{:S(2)}) collective-permute-start(f32[2,1,5,4,256]{4,2,3,0,1:T(8,128)S(1)} %get-tuple-element.423), channel_id=1, source_target_pairs={{0,1},{1,2},{2,3},{3,4},{4,5},{5,6},{6,7},{7,8},{8,9},{9,10},{10,1... | collective-permute-start | bytes 122888 | tf_op jit(solution)/shard_map/while/body/eval_jaxpr/while/body/eval_jaxpr/ppermute | solution.py:20
  255.1 6.8 %collective-permute-start.1 = (f32[2,1,5,4,256]{4,2,3,0,1:T(8,128)S(1)}, f32[2,1,5,4,256]{4,2,3,0,1:T(8,128)S(1)}, u32[]{:S(2)}, u32[]{:S(2)}) collective-permute-start(f32[2,1,5,4,256]{4,2,3,0,1:T(8,128)S(1)} %get-tuple-element.424), channel_id=1, source_target_pairs={{1,0},{2,1},{3,2},{4,3},{5,4},{6,5},{7,6},{8,7},{9,8},{10,9},{11,1... | collective-permute-start | bytes 122888 | tf_op jit(solution)/shard_map/while/body/eval_jaxpr/while/body/eval_jaxpr/ppermute | solution.py:21
  275.3 9.1 %collective-permute-start = (f32[2,1,5,4,256]{4,2,3,0,1:T(8,128)S(1)}, f32[2,1,5,4,256]{4,2,3,0,1:T(8,128)S(1)}, u32[]{:S(2)}, u32[]{:S(2)}) collective-permute-start(f32[2,1,5,4,256]{4,2,3,0,1:T(8,128)S(1)} %get-tuple-element.423), channel_id=1, source_target_pairs={{0,1},{1,2},{2,3},{3,4},{4,5},{5,6},{6,7},{7,8},{8,9},{9,10},{10,1... | collective-permute-start | bytes 122888 | tf_op jit(solution)/shard_map/while/body/eval_jaxpr/while/body/eval_jaxpr/ppermute | solution.py:20
  278.9 6.8 %collective-permute-start.1 = (f32[2,1,5,4,256]{4,2,3,0,1:T(8,128)S(1)}, f32[2,1,5,4,256]{4,2,3,0,1:T(8,128)S(1)}, u32[]{:S(2)}, u32[]{:S(2)}) collective-permute-start(f32[2,1,5,4,256]{4,2,3,0,1:T(8,128)S(1)} %get-tuple-element.424), channel_id=1, source_target_pairs={{1,0},{2,1},{3,2},{4,3},{5,4},{6,5},{7,6},{8,7},{9,8},{10,9},{11,1... | collective-permute-start | bytes 122888 | tf_op jit(solution)/shard_map/while/body/eval_jaxpr/while/body/eval_jaxpr/ppermute | solution.py:21
  299.1 9.1 %collective-permute-start = (f32[2,1,5,4,256]{4,2,3,0,1:T(8,128)S(1)}, f32[2,1,5,4,256]{4,2,3,0,1:T(8,128)S(1)}, u32[]{:S(2)}, u32[]{:S(2)}) collective-permute-start(f32[2,1,5,4,256]{4,2,3,0,1:T(8,128)S(1)} %get-tuple-element.423), channel_id=1, source_target_pairs={{0,1},{1,2},{2,3},{3,4},{4,5},{5,6},{6,7},{7,8},{8,9},{9,10},{10,1... | collective-permute-start | bytes 122888 | tf_op jit(solution)/shard_map/while/body/eval_jaxpr/while/body/eval_jaxpr/ppermute | solution.py:20
  302.7 6.8 %collective-permute-start.1 = (f32[2,1,5,4,256]{4,2,3,0,1:T(8,128)S(1)}, f32[2,1,5,4,256]{4,2,3,0,1:T(8,128)S(1)}, u32[]{:S(2)}, u32[]{:S(2)}) collective-permute-start(f32[2,1,5,4,256]{4,2,3,0,1:T(8,128)S(1)} %get-tuple-element.424), channel_id=1, source_target_pairs={{1,0},{2,1},{3,2},{4,3},{5,4},{6,5},{7,6},{8,7},{9,8},{10,9},{11,1... | collective-permute-start | bytes 122888 | tf_op jit(solution)/shard_map/while/body/eval_jaxpr/while/body/eval_jaxpr/ppermute | solution.py:21
  322.9 9.1 %collective-permute-start = (f32[2,1,5,4,256]{4,2,3,0,1:T(8,128)S(1)}, f32[2,1,5,4,256]{4,2,3,0,1:T(8,128)S(1)}, u32[]{:S(2)}, u32[]{:S(2)}) collective-permute-start(f32[2,1,5,4,256]{4,2,3,0,1:T(8,128)S(1)} %get-tuple-element.423), channel_id=1, source_target_pairs={{0,1},{1,2},{2,3},{3,4},{4,5},{5,6},{6,7},{7,8},{8,9},{9,10},{10,1... | collective-permute-start | bytes 122888 | tf_op jit(solution)/shard_map/while/body/eval_jaxpr/while/body/eval_jaxpr/ppermute | solution.py:20
  326.5 6.8 %collective-permute-start.1 = (f32[2,1,5,4,256]{4,2,3,0,1:T(8,128)S(1)}, f32[2,1,5,4,256]{4,2,3,0,1:T(8,128)S(1)}, u32[]{:S(2)}, u32[]{:S(2)}) collective-permute-start(f32[2,1,5,4,256]{4,2,3,0,1:T(8,128)S(1)} %get-tuple-element.424), channel_id=1, source_target_pairs={{1,0},{2,1},{3,2},{4,3},{5,4},{6,5},{7,6},{8,7},{9,8},{10,9},{11,1... | collective-permute-start | bytes 122888 | tf_op jit(solution)/shard_map/while/body/eval_jaxpr/while/body/eval_jaxpr/ppermute | solution.py:21
  346.7 9.1 %collective-permute-start = (f32[2,1,5,4,256]{4,2,3,0,1:T(8,128)S(1)}, f32[2,1,5,4,256]{4,2,3,0,1:T(8,128)S(1)}, u32[]{:S(2)}, u32[]{:S(2)}) collective-permute-start(f32[2,1,5,4,256]{4,2,3,0,1:T(8,128)S(1)} %get-tuple-element.423), channel_id=1, source_target_pairs={{0,1},{1,2},{2,3},{3,4},{4,5},{5,6},{6,7},{7,8},{8,9},{9,10},{10,1... | collective-permute-start | bytes 122888 | tf_op jit(solution)/shard_map/while/body/eval_jaxpr/while/body/eval_jaxpr/ppermute | solution.py:20
  350.3 6.8 %collective-permute-start.1 = (f32[2,1,5,4,256]{4,2,3,0,1:T(8,128)S(1)}, f32[2,1,5,4,256]{4,2,3,0,1:T(8,128)S(1)}, u32[]{:S(2)}, u32[]{:S(2)}) collective-permute-start(f32[2,1,5,4,256]{4,2,3,0,1:T(8,128)S(1)} %get-tuple-element.424), channel_id=1, source_target_pairs={{1,0},{2,1},{3,2},{4,3},{5,4},{6,5},{7,6},{8,7},{9,8},{10,9},{11,1... | collective-permute-start | bytes 122888 | tf_op jit(solution)/shard_map/while/body/eval_jaxpr/while/body/eval_jaxpr/ppermute | solution.py:21
  370.4 9.1 %collective-permute-start = (f32[2,1,5,4,256]{4,2,3,0,1:T(8,128)S(1)}, f32[2,1,5,4,256]{4,2,3,0,1:T(8,128)S(1)}, u32[]{:S(2)}, u32[]{:S(2)}) collective-permute-start(f32[2,1,5,4,256]{4,2,3,0,1:T(8,128)S(1)} %get-tuple-element.423), channel_id=1, source_target_pairs={{0,1},{1,2},{2,3},{3,4},{4,5},{5,6},{6,7},{7,8},{8,9},{9,10},{10,1... | collective-permute-start | bytes 122888 | tf_op jit(solution)/shard_map/while/body/eval_jaxpr/while/body/eval_jaxpr/ppermute | solution.py:20
  374.0 6.8 %collective-permute-start.1 = (f32[2,1,5,4,256]{4,2,3,0,1:T(8,128)S(1)}, f32[2,1,5,4,256]{4,2,3,0,1:T(8,128)S(1)}, u32[]{:S(2)}, u32[]{:S(2)}) collective-permute-start(f32[2,1,5,4,256]{4,2,3,0,1:T(8,128)S(1)} %get-tuple-element.424), channel_id=1, source_target_pairs={{1,0},{2,1},{3,2},{4,3},{5,4},{6,5},{7,6},{8,7},{9,8},{10,9},{11,1... | collective-permute-start | bytes 122888 | tf_op jit(solution)/shard_map/while/body/eval_jaxpr/while/body/eval_jaxpr/ppermute | solution.py:21
  394.2 9.1 %collective-permute-start = (f32[2,1,5,4,256]{4,2,3,0,1:T(8,128)S(1)}, f32[2,1,5,4,256]{4,2,3,0,1:T(8,128)S(1)}, u32[]{:S(2)}, u32[]{:S(2)}) collective-permute-start(f32[2,1,5,4,256]{4,2,3,0,1:T(8,128)S(1)} %get-tuple-element.423), channel_id=1, source_target_pairs={{0,1},{1,2},{2,3},{3,4},{4,5},{5,6},{6,7},{7,8},{8,9},{9,10},{10,1... | collective-permute-start | bytes 122888 | tf_op jit(solution)/shard_map/while/body/eval_jaxpr/while/body/eval_jaxpr/ppermute | solution.py:20
  397.8 6.8 %collective-permute-start.1 = (f32[2,1,5,4,256]{4,2,3,0,1:T(8,128)S(1)}, f32[2,1,5,4,256]{4,2,3,0,1:T(8,128)S(1)}, u32[]{:S(2)}, u32[]{:S(2)}) collective-permute-start(f32[2,1,5,4,256]{4,2,3,0,1:T(8,128)S(1)} %get-tuple-element.424), channel_id=1, source_target_pairs={{1,0},{2,1},{3,2},{4,3},{5,4},{6,5},{7,6},{8,7},{9,8},{10,9},{11,1... | collective-permute-start | bytes 122888 | tf_op jit(solution)/shard_map/while/body/eval_jaxpr/while/body/eval_jaxpr/ppermute | solution.py:21
where the time goes:
time: 445 us; the launch traced here: 442 us
  starting transfers between devices  101 us (23%)
  other arithmetic  98.7 us (22%)
  local copies, waits for them, and re-layouts  95.3 us (21%)
  matrix products  50.4 us (11%)
  blocking collectives  39.6 us (9%)
  loops' own time  34.8 us (8%)
  waiting for transfers between devices  20.6 us (5%)
    ppermute x17, starting transfers between devices, with_halo(): before = lax.ppermute(last, axis, up)  68.7 us
    dot_general x64, matrix products, apply_operator(): jnp.einsum('kvw,krfwyz->rfvyz', operators, stencil, precision=lax.Precisi...  49.4 us
    mul x64, other arithmetic, apply_operator(): turning = jnp.stack([spinning * center[1], -spinning * center[0]])  44.4 us
    another operation x1, loops' own time, on_device(): lax.scan(group_march, own_inflow, jnp.arange(stream_count, dtype=jnp.int32))  34.8 us
    ppermute x17, starting transfers between devices, with_halo(): after = lax.ppermute(first, axis, down)  32.6 us
    mul x32, other arithmetic, recursion(): current = refreshed * inside[row_start:row_stop][:, None]  23.4 us
    all_to_all x1, blocking collectives, on_device(): lax.all_to_all(exits, 'stream', split_axis=0, concat_axis=2, tiled=True)  23.3 us
    ppermute x17, waiting for transfers between devices, with_halo(): after = lax.ppermute(first, axis, down)  20.5 us
  transfers between devices with their start and end apart: 34, of which 16 were waited for; matrix products, arithmetic and copies ran while one was open for 7% of the time, Pallas kernels for 0%

commit v1 on v0

v1 whole, which is shorter than its diff:
```python
import functools

import jax
import jax.numpy as jnp
from jax import lax
from jax.experimental import pallas as pl
from jax.experimental.pallas import tpu as pltpu
from jax.sharding import PartitionSpec as P

viscosity = 0.05
penalty = 0.5
damping = 0.03

MESH = pl.DeviceIdType.MESH
ROWS = 8
OWN = 4
PAIRS = 12
STEP = 2


def kernel(
    dims,
    inflow,
    shape,
    amp,
    coupling,
    omega,
    rec_coef,
    rec_order,
    zone,
    mask,
    out,
    nat_in,
    shape_in,
    mask_in,
    tile,
    amp_all,
    zone_all,
    coef,
    diag,
    field,
    frame_src,
    frame_damp,
    sent,
    got,
    sent_fix,
    got_fix,
    exits,
    in_sem,
    gather_send,
    gather_recv,
    halo_send,
    halo_recv,
    fix_send,
    fix_recv,
    exit_send,
    exit_recv,
    local_sem,
):
    streams, crosses, freqs, nvar, zones, stations = dims
    me = lax.axis_index("stream")
    row = lax.axis_index("cross")
    freq = lax.rem(me, freqs)
    part = lax.div(me, freqs)
    above = row > 0
    below = row < crosses - 1

    sub = lax.broadcasted_iota(jnp.int32, (8, 128), 0)
    lane = lax.broadcasted_iota(jnp.int32, (8, 128), 1)
    top = (sub & 2) == 0
    real = (sub & 1) == 0
    first = lane == 0
    last = lane == 127

    def swap_rows(x):
        return jnp.where(top, pltpu.roll(x, 6, 0), pltpu.roll(x, 2, 0))

    def swap_parts(x):
        return jnp.where(real, pltpu.roll(x, 7, 0), pltpu.roll(x, 1, 0))

    loads = [
        pltpu.make_async_copy(inflow.at[:, freq], nat_in, in_sem.at[0]),
        pltpu.make_async_copy(shape, shape_in, in_sem.at[1]),
        pltpu.make_async_copy(mask, mask_in, in_sem.at[2]),
        pltpu.make_async_copy(amp.at[0], amp_all.at[me], in_sem.at[3]),
        pltpu.make_async_copy(zone, zone_all.at[me], in_sem.at[4]),
    ]
    for load in loads:
        load.start()

    barrier = pltpu.get_barrier_semaphore()

    def greet(k, carry):
        pl.semaphore_signal(
            barrier,
            inc=1,
            device_id=(lax.rem(me + k, streams), row),
            device_id_type=MESH,
        )
        return carry

    @pl.when(above)
    def _():
        pl.semaphore_signal(barrier, inc=1, device_id=(me, row - 1), device_id_type=MESH)

    @pl.when(below)
    def _():
        pl.semaphore_signal(barrier, inc=1, device_id=(me, row + 1), device_id_type=MESH)

    lax.fori_loop(1, streams, greet, 0)

    @pl.when(row == 0)
    def _():
        got[0, 0] = jnp.zeros_like(got[0, 0])
        got[1, 0] = jnp.zeros_like(got[1, 0])
        got_fix[0] = jnp.zeros_like(got_fix[0])

    @pl.when(row == crosses - 1)
    def _():
        got[0, 1] = jnp.zeros_like(got[0, 1])
        got[1, 1] = jnp.zeros_like(got[1, 1])
        got_fix[1] = jnp.zeros_like(got_fix[1])

    per_zone = 4 * nvar * nvar
    side = jnp.where(top, 1.0, -1.0).astype(jnp.float32)

    def zone_coef(z, carry):
        def put(kind, i, w, value):
            coef[z * per_zone + (kind * nvar + i) * nvar + w] = value

        def full(value):
            return jnp.full((8, 128), value, jnp.float32)

        for i in range(nvar):
            for w in range(i, nvar):
                rows_iw = full(0.25 * (coupling[z, 0, i, w] + coupling[z, 0, w, i])) * side
                cols_iw = full(0.25 * (coupling[z, 1, i, w] + coupling[z, 1, w, i]))
                dot = coupling[z, 3, i, 0] * coupling[z, 3, w, 0]
                for k in range(1, nvar):
                    dot = dot + coupling[z, 3, i, k] * coupling[z, 3, w, k]
                if i == w:
                    dot = dot + 1.0
                visc = viscosity * dot
                turn = 0.5 * (coupling[z, 2, i, w] - coupling[z, 2, w, i])
                put(0, i, w, rows_iw)
                put(1, i, w, cols_iw)
                put(3, i, w, full(visc))
                put(2, i, w, full(turn - 4.0 * visc))
                if i != w:
                    put(0, w, i, rows_iw)
                    put(1, w, i, cols_iw)
                    put(3, w, i, full(visc))
                    put(2, w, i, full(-turn - 4.0 * visc))
        return carry

    lax.fori_loop(0, zones, zone_coef, 0)

    f0, f1, f2, f3 = [rec_coef[rec_order[k]] * (1.0 / (4 - k)) for k in range(4)]
    spin = omega[freq]
    c1 = f3
    c2 = c1 * f2
    c3 = c2 * f1
    c4 = c3 * f0
    spin2 = spin * spin
    spin3 = spin2 * spin
    re_part = [1.0 - c2 * spin2 + c4 * spin2 * spin2, c1 - 3.0 * c3 * spin2, c2 - 6.0 * c4 * spin2, c3, c4]
    im_part = [c3 * spin3 - c1 * spin, 4.0 * c4 * spin3 - 2.0 * c2 * spin, -3.0 * c3 * spin, -4.0 * c4 * spin]
    flip = jnp.where(real, 1.0, -1.0).astype(jnp.float32)
    for k in range(5):
        coef[zones * per_zone + k] = jnp.full((8, 128), re_part[k], jnp.float32)
    for k in range(4):
        coef[zones * per_zone + 5 + k] = jnp.full((8, 128), im_part[k], jnp.float32) * flip

    def pairs_of(slot, get):
        for p in range(2):
            for h in range(2):
                tile[slot, pl.ds(4 * h + p, 8, stride=8), :] = get(p, h)
        return [
            jnp.where(top, tile[slot, 8 * k : 8 * k + 8], swap_rows(tile[slot, 56 - 8 * k : 64 - 8 * k]))
            for k in range(OWN)
        ]

    for load in loads:
        load.wait()
    for v in range(nvar):
        own = pairs_of(v, lambda p, h: nat_in[p, v, :, 128 * h : 128 * h + 128])
        for k in range(OWN):
            field[0, v, 8 + k] = own[k]
            sent[0, v * OWN + k] = own[k]
    for v in range(nvar):
        own = pairs_of(v, lambda p, h: shape_in[v, :, 128 * h : 128 * h + 128])
        for k in range(OWN):
            frame_src[v, 8 + k] = own[k]
            sent_fix[v * OWN + k] = own[k]
    own = pairs_of(
        0,
        lambda p, h: penalty * mask_in[:, 128 * h : 128 * h + 128].astype(jnp.float32) + damping,
    )
    for k in range(OWN):
        frame_damp[8 + k] = own[k]
        sent_fix[nvar * OWN + k] = own[k]

    pl.semaphore_wait(barrier, streams - 1 + above.astype(jnp.int32) + below.astype(jnp.int32))

    def gather_copies(k):
        peer = lax.rem(me + k, streams)
        return (
            pltpu.make_async_remote_copy(
                zone, zone_all.at[me], gather_send.at[0, k], gather_recv.at[0, k],
                device_id=(peer, row), device_id_type=MESH,
            ),
            pltpu.make_async_remote_copy(
                amp.at[0], amp_all.at[me], gather_send.at[1, k], gather_recv.at[1, k],
                device_id=(peer, row), device_id_type=MESH,
            ),
        )

    def gather_start(k, carry):
        for copy in gather_copies(k):
            copy.start()
        return carry

    lax.fori_loop(1, streams, gather_start, 0)

    def halo_copies(exchange, slot):
        up = pltpu.make_async_remote_copy(
            sent.at[slot], got.at[slot, 1], halo_send.at[slot, 0], halo_recv.at[slot, 1],
            device_id=(me, row - 1), device_id_type=MESH,
        )
        down = pltpu.make_async_remote_copy(
            sent.at[slot], got.at[slot, 0], halo_send.at[slot, 1], halo_recv.at[slot, 0],
            device_id=(me, row + 1), device_id_type=MESH,
        )
        return up, down

    fix_up = pltpu.make_async_remote_copy(
        sent_fix, got_fix.at[1], fix_send.at[0], fix_recv.at[1],
        device_id=(me, row - 1), device_id_type=MESH,
    )
    fix_down = pltpu.make_async_remote_copy(
        sent_fix, got_fix.at[0], fix_send.at[1], fix_recv.at[0],
        device_id=(me, row + 1), device_id_type=MESH,
    )

    def halo_start(exchange, slot):
        up, down = halo_copies(exchange, slot)

        @pl.when(above)
        def _():
            up.start()

        @pl.when(below)
        def _():
            down.start()

    def halo_wait_send(slot):
        up, down = halo_copies(0, slot)

        @pl.when(above)
        def _():
            up.wait_send()

        @pl.when(below)
        def _():
            down.wait_send()

    def halo_wait_recv(slot):
        up, down = halo_copies(0, slot)

        @pl.when(above)
        def _():
            down.wait_recv()

        @pl.when(below)
        def _():
            up.wait_recv()

    @pl.when(above)
    def _():
        fix_up.start()

    @pl.when(below)
    def _():
        fix_down.start()

    halo_start(0, 0)

    def halo_pairs(before, after):
        outer = [jnp.where(top, before(k), after(k)) for k in range(OWN)]
        inner = [swap_rows(jnp.where(top, after(k), before(k))) for k in range(OWN)]
        return outer + inner[::-1]

    @pl.when(above)
    def _():
        fix_up.wait_send()
        fix_down.wait_recv()

    @pl.when(below)
    def _():
        fix_down.wait_send()
        fix_up.wait_recv()

    for v in range(nvar):
        halo = halo_pairs(lambda k: got_fix[0, v * OWN + k], lambda k: got_fix[1, v * OWN + k])
        for j in range(8):
            frame_src[v, j] = halo[j]
    halo = halo_pairs(
        lambda k: got_fix[0, nvar * OWN + k], lambda k: got_fix[1, nvar * OWN + k]
    )
    for j in range(8):
        frame_damp[j] = halo[j]

    def zone_diag(z, carry):
        for i in range(nvar):
            center = coef[z * per_zone + (2 * nvar + i) * nvar + i]
            for j in range(1, PAIRS):
                diag[(z * nvar + i) * PAIRS + j] = center - frame_damp[j]
        return carry

    lax.fori_loop(0, zones, zone_diag, 0)

    inside = jnp.where(top, above.astype(jnp.float32), below.astype(jnp.float32))

    def gather_wait(k, carry):
        for copy in gather_copies(k):
            copy.wait()
        return carry

    lax.fori_loop(1, streams, gather_wait, 0)

    def exit_copy(n):
        return pltpu.make_async_remote_copy(
            exits.at[n], out.at[0, part, freq], exit_send.at[n], exit_recv.at[me],
            device_id=(n, row), device_id_type=MESH,
        )

    def exit_local(n):
        return pltpu.make_async_copy(exits.at[n], out.at[0, part, freq], local_sem)

    def march(n, start):
        here = jnp.max(zone_all[n])
        base = here * per_zone
        dbase = here * (nvar * PAIRS)
        amps = amp_all[n]
        mine = lax.broadcasted_iota(jnp.int32, amps.shape, 1) == freq
        amps = jnp.sum(jnp.where(mine, amps, 0.0), axis=1, keepdims=True)
        weight = jnp.where(real, amps[0:1], amps[1:2])
        for level in range(4):
            lo = start + 1 + level
            js = list(range(lo, PAIRS))
            chunks = [js[a : a + 2] for a in range(len(js) % 2 and 1 or 0, len(js), 2)]
            if len(js) % 2:
                chunks = [js[:1]] + chunks
            for chunk in chunks:
                feats = {}
                for v in range(nvar):
                    vs = {
                        j: field[level, v, j] for j in range(chunk[0] - 1, chunk[-1] + 2)
                    }
                    for j in chunk:
                        x = vs[j]
                        other = pltpu.roll(x, 4, 0)
                        east = pltpu.roll(jnp.where(first, other, x), 127, 1)
                        west = pltpu.roll(jnp.where(last, other, x), 1, 1)
                        feats[v, j] = (
                            vs[j + 1] - vs[j - 1],
                            east - west,
                            x,
                            (vs[j + 1] + vs[j - 1]) + (east + west),
                        )
                for i in range(nvar):
                    total = {
                        j: diag[dbase + i * PAIRS + j] * feats[i, j][2] for j in chunk
                    }
                    for kind in range(4):
                        for w in range(nvar):
                            if kind == 2 and w == i:
                                continue
                            g = coef[base + (kind * nvar + i) * nvar + w]
                            for j in chunk:
                                total[j] = total[j] + g * feats[w, j][kind]
                    for j in chunk:
                        value = total[j]
                        if j == 7:
                            value = value * inside
                        if level < 3:
                            field[level + 1, i, j] = value
                            if j == PAIRS - 1:
                                field[level + 1, i, PAIRS] = swap_rows(value)
                        else:
                            u = [field[k, i, j] for k in range(4)]
                            b = zones * per_zone
                            a_sum = coef[b] * u[0] + coef[b + 4] * value
                            b_sum = coef[b + 5] * u[0]
                            for k in range(1, 4):
                                a_sum = a_sum + coef[b + k] * u[k]
                                b_sum = b_sum + coef[b + 5 + k] * u[k]
                            new = a_sum + swap_parts(b_sum) + weight * frame_src[i, j]
                            field[0, i, j] = new
                            if j == PAIRS - 1:
                                field[0, i, PAIRS] = swap_rows(new)

    def leave(n):
        for v in range(nvar):
            for k in range(OWN):
                x = field[0, v, 8 + k]
                tile[v, 8 * k : 8 * k + 8] = x
                tile[v, 56 - 8 * k : 64 - 8 * k] = swap_rows(x)
            for h in range(2):
                even = tile[v, pl.ds(4 * h, 8, stride=8), :]
                odd = tile[v, pl.ds(4 * h + 1, 8, stride=8), :]
                exits[n, v, :, 128 * h : 128 * h + 128] = jnp.where(part == 0, even, odd)

        @pl.when(n == me)
        def _():
            exit_local(n).start()

        @pl.when(n != me)
        def _():
            exit_copy(n).start()

    for v in range(nvar):
        field[0, v, PAIRS] = swap_rows(field[0, v, PAIRS - 1])

    stages = stations // STEP

    def stage(t, carry):
        slot = lax.rem(t, 2)
        other = 1 - slot
        halo_wait_recv(slot)
        for v in range(nvar):
            halo = halo_pairs(lambda k: got[slot, 0, v * OWN + k], lambda k: got[slot, 1, v * OWN + k])
            for j in range(8):
                field[0, v, j] = halo[j]
        march(2 * t, 0)
        leave(2 * t)
        march(2 * t + 1, 4)

        @pl.when(t < stages - 1)
        def _():
            @pl.when(t > 0)
            def _():
                halo_wait_send(other)

            for v in range(nvar):
                for k in range(OWN):
                    sent[other, v * OWN + k] = field[0, v, 8 + k]
            halo_start(t + 1, other)

        leave(2 * t + 1)
        return carry

    lax.fori_loop(0, stages, stage, 0)

    if stages > 1:
        halo_wait_send((stages - 2) % 2)
    halo_wait_send((stages - 1) % 2)

    def finish(n, carry):
        @pl.when(n == me)
        def _():
            exit_local(n).wait()

        @pl.when(n != me)
        def _():
            exit_copy(n).wait_send()
            pltpu.make_async_remote_copy(
                exits.at[n], out.at[0, part, freq], exit_send.at[n], exit_recv.at[n],
                device_id=(n, row), device_id_type=MESH,
            ).wait_recv()

        return carry

    lax.fori_loop(0, streams, finish, 0)


def on_device(dims, inflow, shape, amp, coupling, omega, rec_coef, rec_order, zone, mask):
    streams, crosses, freqs, nvar, zones, stations = dims
    cols = inflow.shape[-1]
    anywhere = pl.BlockSpec(memory_space=pl.ANY)
    scalars = pl.BlockSpec(memory_space=pltpu.SMEM)
    f32 = jnp.float32
    dma = pltpu.SemaphoreType.DMA
    return pl.pallas_call(
        functools.partial(kernel, dims),
        out_shape=jax.ShapeDtypeStruct((1, 2, freqs, nvar, ROWS, cols), f32),
        in_specs=[anywhere, anywhere, anywhere, scalars, scalars, scalars, scalars, anywhere, anywhere],
        out_specs=anywhere,
        scratch_shapes=[
            pltpu.VMEM((2, nvar, ROWS, cols), f32),
            pltpu.VMEM((nvar, ROWS, cols), f32),
            pltpu.VMEM((ROWS, cols), jnp.int32),
            pltpu.VMEM((nvar, 64, 128), f32),
            pltpu.VMEM((streams, 2, freqs), f32),
            pltpu.VMEM((streams, 1, 1), jnp.int32),
            pltpu.VMEM((zones * 4 * nvar * nvar + 9, 8, 128), f32),
            pltpu.VMEM((zones * nvar * PAIRS, 8, 128), f32),
            pltpu.VMEM((4, nvar, PAIRS + 1, 8, 128), f32),
            pltpu.VMEM((nvar, PAIRS, 8, 128), f32),
            pltpu.VMEM((PAIRS, 8, 128), f32),
            pltpu.VMEM((2, nvar * OWN, 8, 128), f32),
            pltpu.VMEM((2, 2, nvar * OWN, 8, 128), f32),
            pltpu.VMEM(((nvar + 1) * OWN, 8, 128), f32),
            pltpu.VMEM((2, (nvar + 1) * OWN, 8, 128), f32),
            pltpu.VMEM((streams, nvar, ROWS, cols), f32),
            dma((5,)),
            dma((2, streams)),
            dma((2, streams)),
            dma((2, 2)),
            dma((2, 2)),
            dma((2,)),
            dma((2,)),
            dma((streams,)),
            dma((streams,)),
            dma,
        ],
        compiler_params=pltpu.CompilerParams(collective_id=0, has_side_effects=True),
        name="march",
    )(inflow, shape, amp, coupling, omega, rec_coef, rec_order, zone.reshape(1, 1), mask)


def solution(mesh):
    placed = (
        P(None, None, None, "cross", None),
        P(None, "cross", None),
        P("stream", None, None),
        P(),
        P(),
        P(),
        P(),
        P("stream"),
        P("cross", None),
    )

    def whole(inflow, source_shape, source_amp, coupling, omega, rec_coef, rec_order, station_zone, solid_mask):
        streams = mesh.shape["stream"]
        crosses = mesh.shape["cross"]
        dims = (
            streams,
            crosses,
            inflow.shape[1],
            inflow.shape[2],
            coupling.shape[0],
            station_zone.shape[0],
        )
        return jax.shard_map(
            functools.partial(on_device, dims),
            mesh=mesh,
            in_specs=placed,
            out_specs=P("stream", None, None, None, "cross", None),
            check_vma=False,
        )(inflow, source_shape, source_amp, coupling, omega, rec_coef, rec_order, station_zone, solid_mask)

    return whole
```

time: 445 us -> 72.4 us (0.16)
  the two profiles are of different devices: /device:TPU:97 before, /device:TPU:255 now
where the time goes in v1:
time: 72.4 us; the launch traced here: 72.1 us
  Pallas kernels  68 us (94%)
  local copies, waits for them, and re-layouts  3.4 us (5%)
    pallas_call x1, Pallas kernels, on_device(): pl.pallas_call(functools.partial(kernel, dims), out_shape=jax.ShapeDtypeS...  68 us
    unnamed x2, local copies, waits for them, and re-layouts  3.4 us

profile of v1, /device:TPU:255, one launch (start us, length us, event | category | flops | bytes accessed | tf_op | source)
XLA Modules:
  0.0 72.1 jit_solution(7204356792783486807)
XLA Ops:
  0.7 1.4 %copy.10.coupling = f32[4,4,5,5]{3,2,1,0:T(8,128)} copy(f32[4,4,5,5]{3,1,2,0:T(4,128)} %param.12) | data formatting | bytes 3200 | tf_op args[3]
  2.1 68.0 %march.1 = f32[1,2,8,5,8,256]{5,4,3,2,1,0:T(8,128)} custom-call(f32[2,8,5,8,256]{4,3,2,1,0:T(8,128)} %inflow.1, f32[5,8,256]{2,1,0:T(8,128)} %shape.1, f32[1,2,8]{2,1,0:T(2,128)} %amp.1, f32[4,4,5,5]{3,2,1,0:T(8,128)} %copy.10.coupling, f32[8]{0:T(128)} %omega.1, f32[4]{0:T(128)} %rec_coef.1, s32[4]{0:T(128)} %rec_order.1, s32[1,1]{1,0:T(1,128)} %bitcast.1.zone, ...), custom_call_target="tpu_custom_call" | custom-call | tf_op jit(solution)/shard_map/march/pallas_call | solution.py:484
  70.1 2.0 %copy.13 = f32[1,2,8,5,8,256]{5,4,3,2,1,0:T(8,128)} copy(f32[1,2,8,5,8,256]{5,4,3,2,1,0:T(8,128)} %march.1) | data formatting | bytes 1310720

commit v2 on v1

v2 whole, which is shorter than its diff:
```python
import functools

import jax
import jax.numpy as jnp
from jax import lax
from jax.experimental import pallas as pl
from jax.experimental.pallas import tpu as pltpu
from jax.sharding import PartitionSpec as P

viscosity = 0.05
penalty = 0.5
damping = 0.03

MESH = pl.DeviceIdType.MESH
ROWS = 8
OWN = 4
RECUR = 4
REACH = 2
STEP = REACH * ROWS // RECUR
LEVELS = STEP * RECUR
HERE = 8 * REACH
PAIRS = HERE + OWN
SIDE = 4
ORDER = (0, 1, 0, 1, 2, 3, 2, 3, 4, 4)


def kernel(
    dims,
    inflow,
    shape,
    amp,
    coupling_in,
    omega,
    rec_coef,
    rec_order,
    zone,
    mask,
    out,
    nat_in,
    shape_in,
    mask_in,
    coupling,
    tile,
    amp_all,
    zone_all,
    mix32,
    mix,
    coef,
    field,
    packed,
    frame_src,
    frame_damp,
    sent,
    got,
    sent_fix,
    got_fix,
    exits,
    in_sem,
    gather_send,
    gather_recv,
    halo_send,
    halo_recv,
    fix_send,
    fix_recv,
    exit_send,
    exit_recv,
    local_sem,
):
    streams, crosses, freqs, nvar, zones, stations = dims
    me = lax.axis_index("stream")
    row = lax.axis_index("cross")
    freq = lax.div(me, SIDE) * 2 + lax.rem(me, 2)
    part = lax.rem(lax.div(me, 2), 2)
    above = [row >= n for n in range(1, REACH + 1)]
    below = [row < crosses - n for n in range(1, REACH + 1)]

    sub = lax.broadcasted_iota(jnp.int32, (8, 128), 0)
    lane = lax.broadcasted_iota(jnp.int32, (8, 128), 1)
    top = (sub & 2) == 0
    real = (sub & 1) == 0
    first = lane == 0
    last = lane == 127

    def swap_rows(x):
        return jnp.where(top, pltpu.roll(x, 6, 0), pltpu.roll(x, 2, 0))

    def swap_parts(x):
        return jnp.where(real, pltpu.roll(x, 7, 0), pltpu.roll(x, 1, 0))

    loads = [
        pltpu.make_async_copy(inflow.at[:, freq], nat_in, in_sem.at[0]),
        pltpu.make_async_copy(shape, shape_in, in_sem.at[1]),
        pltpu.make_async_copy(mask, mask_in, in_sem.at[2]),
        pltpu.make_async_copy(amp.at[0], amp_all.at[me], in_sem.at[3]),
        pltpu.make_async_copy(zone, zone_all.at[me], in_sem.at[4]),
        pltpu.make_async_copy(coupling_in, coupling, in_sem.at[5]),
    ]
    for load in loads:
        load.start()

    barrier = pltpu.get_barrier_semaphore()

    def greet(k, carry):
        pl.semaphore_signal(
            barrier,
            inc=1,
            device_id=(lax.rem(me + k, streams), row),
            device_id_type=MESH,
        )
        return carry

    for n in range(REACH):

        @pl.when(above[n])
        def _():
            pl.semaphore_signal(barrier, inc=1, device_id=(me, row - 1 - n), device_id_type=MESH)

        @pl.when(below[n])
        def _():
            pl.semaphore_signal(barrier, inc=1, device_id=(me, row + 1 + n), device_id_type=MESH)

    lax.fori_loop(1, streams, greet, 0)

    for n in range(REACH):
        for missing, at in ((~above[n], 0), (~below[n], 1)):

            @pl.when(missing)
            def _():
                for slot in range(2):
                    got[slot, n, at] = jnp.zeros_like(got[slot, n, at])
                got_fix[n, at] = jnp.zeros_like(got_fix[n, at])

    side = jnp.where(top, 1.0, -1.0).astype(jnp.float32)
    same = (lane & 7) == sub
    spots = {}
    for kind in range(3):
        for w in range(nvar):
            for t in range(2):
                eights = [
                    10 * kind + g - 16 * t
                    for g in range(10)
                    if ORDER[g] == w and 0 <= 10 * kind + g - 16 * t < 16
                ]
                if eights:
                    hit = functools.reduce(
                        jnp.logical_or, [lax.shift_right_logical(lane, 3) == g for g in eights]
                    )
                    spots[kind, w, t] = hit & same

    loads[5].wait()

    def zone_mix(z, carry):
        def full(value):
            return jnp.full((8, 128), value, jnp.float32)

        table = {}
        for i in range(nvar):
            for w in range(i, nvar):
                rows_iw = full(0.25 * (coupling[z, 0, i, w] + coupling[z, 0, w, i])) * side
                cols_iw = 0.25 * (coupling[z, 1, i, w] + coupling[z, 1, w, i])
                dot = coupling[z, 3, i, 0] * coupling[z, 3, w, 0]
                for k in range(1, nvar):
                    dot = dot + coupling[z, 3, i, k] * coupling[z, 3, w, k]
                if i == w:
                    dot = dot + 1.0
                visc = viscosity * dot
                turn = 0.5 * (coupling[z, 2, i, w] - coupling[z, 2, w, i])
                around = (visc + rows_iw, visc - rows_iw, full(visc + cols_iw), full(visc - cols_iw))
                table[i, w] = (full(turn - 4.0 * visc),) + around
                table[w, i] = (full(-turn - 4.0 * visc),) + around
        for i in range(nvar):
            for block, kinds in ((0, (0, 1, 2)), (1, (3,)), (2, (4,))):
                for t in range(2):
                    value = jnp.zeros((8, 128), jnp.float32)
                    for place, kind in enumerate(kinds):
                        for w in range(nvar):
                            if (place, w, t) in spots:
                                value = jnp.where(spots[place, w, t], table[i, w][kind], value)
                    high = value.astype(jnp.bfloat16).astype(jnp.float32)
                    at = 8 * (2 * nvar * block + i)
                    mix32[at : at + 8, 128 * t : 128 * t + 128] = high
                    at = at + 8 * nvar
                    mix32[at : at + 8, 128 * t : 128 * t + 128] = value - high
        mix[z] = mix32[...].astype(jnp.bfloat16)
        return carry

    lax.fori_loop(0, zones, zone_mix, 0)

    f0, f1, f2, f3 = [rec_coef[rec_order[k]] * (1.0 / (4 - k)) for k in range(4)]
    spin = omega[freq]
    c1 = f3
    c2 = c1 * f2
    c3 = c2 * f1
    c4 = c3 * f0
    spin2 = spin * spin
    spin3 = spin2 * spin
    re_part = [1.0 - c2 * spin2 + c4 * spin2 * spin2, c1 - 3.0 * c3 * spin2, c2 - 6.0 * c4 * spin2, c3, c4]
    im_part = [c3 * spin3 - c1 * spin, 4.0 * c4 * spin3 - 2.0 * c2 * spin, -3.0 * c3 * spin, -4.0 * c4 * spin]
    flip = jnp.where(real, 1.0, -1.0).astype(jnp.float32)
    for k in range(5):
        coef[k] = jnp.full((8, 128), re_part[k], jnp.float32)
    for k in range(4):
        coef[5 + k] = jnp.full((8, 128), im_part[k], jnp.float32) * flip

    def halves(x, y=None):
        both = x if y is None else jnp.concatenate([x, y], axis=0)
        high = both.astype(jnp.bfloat16)
        wide = high.astype(jnp.float32)
        low = both - wide
        if y is None:
            return jnp.concatenate([wide, low], axis=0).astype(jnp.bfloat16)
        return high, low.astype(jnp.bfloat16)

    def pack(level, j, xs):
        for v in range(0, nvar - 1, 2):
            high, low = halves(xs[v], xs[v + 1])
            packed[level, j, 16 * v : 16 * v + 16] = high
            packed[level, j, 16 * v + 16 : 16 * v + 32] = low
        packed[level, j, 16 * nvar - 16 : 16 * nvar] = halves(xs[nvar - 1])

    def keep(level, j, xs):
        for v in range(nvar):
            field[level, v, j] = xs[v]
        if level < LEVELS:
            pack(level, j, xs)
            if j == PAIRS - 1:
                pack(level, PAIRS, [swap_rows(x) for x in xs])

    def pairs_of(slot, get):
        for p in range(2):
            for h in range(2):
                tile[slot, pl.ds(4 * h + p, 8, stride=8), :] = get(p, h)
        return [
            jnp.where(top, tile[slot, 8 * k : 8 * k + 8], swap_rows(tile[slot, 56 - 8 * k : 64 - 8 * k]))
            for k in range(OWN)
        ]

    for load in loads[:5]:
        load.wait()
    own = [
        pairs_of(v, lambda p, h: nat_in[p, v, :, 128 * h : 128 * h + 128]) for v in range(nvar)
    ]
    for k in range(OWN):
        keep(0, HERE + k, [own[v][k] for v in range(nvar)])
        for v in range(nvar):
            sent[0, k * nvar + v] = own[v][k]
    for v in range(nvar):
        own = pairs_of(v, lambda p, h: shape_in[v, :, 128 * h : 128 * h + 128])
        for k in range(OWN):
            frame_src[v, HERE + k] = own[k]
            sent_fix[v * OWN + k] = own[k]
    own = pairs_of(
        0,
        lambda p, h: penalty * mask_in[:, 128 * h : 128 * h + 128].astype(jnp.float32) + damping,
    )
    for k in range(OWN):
        frame_damp[HERE + k] = own[k]
        sent_fix[nvar * OWN + k] = own[k]

    near = [x.astype(jnp.int32) for x in above + below]
    pl.semaphore_wait(barrier, streams - 1 + functools.reduce(lambda x, y: x + y, near))

    def gather_copies(k):
        peer = lax.rem(me + k, streams)
        return (
            pltpu.make_async_remote_copy(
                zone, zone_all.at[me], gather_send.at[0, k], gather_recv.at[0, k],
                device_id=(peer, row), device_id_type=MESH,
            ),
            pltpu.make_async_remote_copy(
                amp.at[0], amp_all.at[me], gather_send.at[1, k], gather_recv.at[1, k],
                device_id=(peer, row), device_id_type=MESH,
            ),
        )

    def gather_start(k, carry):
        for copy in gather_copies(k):
            copy.start()
        return carry

    lax.fori_loop(1, streams, gather_start, 0)

    def both_ways(source, target, send_sems, recv_sems, n):
        up = pltpu.make_async_remote_copy(
            source, target.at[n, 1], send_sems.at[n, 0], recv_sems.at[n, 1],
            device_id=(me, row - 1 - n), device_id_type=MESH,
        )
        down = pltpu.make_async_remote_copy(
            source, target.at[n, 0], send_sems.at[n, 1], recv_sems.at[n, 0],
            device_id=(me, row + 1 + n), device_id_type=MESH,
        )
        return up, down

    def halo(slot):
        return [
            both_ways(sent.at[slot], got.at[slot], halo_send.at[slot], halo_recv.at[slot], n)
            for n in range(REACH)
        ]

    fixed = [both_ways(sent_fix, got_fix, fix_send, fix_recv, n) for n in range(REACH)]

    def start(copies):
        for n in range(REACH):

            @pl.when(above[n])
            def _():
                copies[n][0].start()

            @pl.when(below[n])
            def _():
                copies[n][1].start()

    def wait_send(copies):
        for n in range(REACH):

            @pl.when(above[n])
            def _():
                copies[n][0].wait_send()

            @pl.when(below[n])
            def _():
                copies[n][1].wait_send()

    def wait_recv(copies):
        for n in range(REACH):

            @pl.when(above[n])
            def _():
                copies[n][1].wait_recv()

            @pl.when(below[n])
            def _():
                copies[n][0].wait_recv()

    start(halo(0))
    start(fixed)

    def halo_pairs(before, after):
        outer = [jnp.where(top, before(k), after(k)) for k in range(OWN)]
        inner = [swap_rows(jnp.where(top, after(k), before(k))) for k in range(OWN)]
        return outer + inner[::-1]

    wait_send(fixed)
    wait_recv(fixed)
    for n in range(REACH):
        base = HERE - 8 * (n + 1)
        for v in range(nvar + 1):
            pairs = halo_pairs(
                lambda k: got_fix[n, 0, v * OWN + k], lambda k: got_fix[n, 1, v * OWN + k]
            )
            for j in range(8):
                if v < nvar:
                    frame_src[v, base + j] = pairs[j]
                else:
                    frame_damp[base + j] = pairs[j]

    inside = {
        HERE - 1 - 8 * n: jnp.where(top, near[n].astype(jnp.float32), near[REACH + n].astype(jnp.float32))
        for n in range(REACH)
    }

    def gather_wait(k, carry):
        for copy in gather_copies(k):
            copy.wait()
        return carry

    lax.fori_loop(1, streams, gather_wait, 0)

    def exit_copy(n, p, source):
        return pltpu.make_async_remote_copy(
            exits.at[n, p], out.at[0, p, freq], exit_send.at[n, p], exit_recv.at[source, p],
            device_id=(n, row), device_id_type=MESH,
        )

    def exit_local(n, p):
        return pltpu.make_async_copy(exits.at[n, p], out.at[0, p, freq], local_sem.at[p])

    spot = lax.rem(me, SIDE)

    def same_line(n):
        return lax.rem(n, SIDE) == spot

    def other_lines(n):
        return lax.rem(n + me, 2) == 1

    def station(n):
        here = jnp.max(zone_all[n])
        amps = amp_all[n]
        mine = lax.broadcasted_iota(jnp.int32, amps.shape, 1) == freq
        amps = jnp.sum(jnp.where(mine, amps, 0.0), axis=1, keepdims=True)
        return here, jnp.where(real, amps[0:1], amps[1:2])

    def task(level, chunk, stations_):
        here, weight = stations_[level // RECUR]
        operands = [
            jnp.concatenate([packed[level, j], packed[level, j + 1], packed[level, j - 1]], axis=0)
            for j in chunk
        ]
        operand = operands[0] if len(chunk) == 1 else jnp.concatenate(operands, axis=1)
        result = jnp.dot(
            mix[here, :, 0 : operand.shape[0]], operand, preferred_element_type=jnp.float32
        )
        base = level // RECUR * RECUR
        for a, j in enumerate(chunk):

            def part_of(block, i):
                at = 8 * (2 * nvar * block + i)
                cols = slice(128 * a, 128 * a + 128)
                return result[at : at + 8, cols] + result[at + 8 * nvar : at + 8 * nvar + 8, cols]

            values = []
            for i in range(nvar):
                east = part_of(1, i)
                west = part_of(2, i)
                east = pltpu.roll(jnp.where(first, pltpu.roll(east, 4, 0), east), 127, 1)
                west = pltpu.roll(jnp.where(last, pltpu.roll(west, 4, 0), west), 1, 1)
                value = part_of(0, i) - frame_damp[j] * field[level, i, j] + (east + west)
                if j in inside:
                    value = value * inside[j]
                if (level + 1) % RECUR == 0:
                    u = [field[base + k, i, j] for k in range(4)]
                    a_sum = coef[0] * u[0] + coef[4] * value
                    b_sum = coef[5] * u[0]
                    for k in range(1, 4):
                        a_sum = a_sum + coef[k] * u[k]
                        b_sum = b_sum + coef[5 + k] * u[k]
                    value = a_sum + swap_parts(b_sum) + weight * frame_src[i, j]
                values.append(value)
            keep(level + 1, j, values)

    def leave(n, level):
        for v in range(nvar):
            for k in range(OWN):
                x = field[level, v, HERE + k]
                tile[v, 8 * k : 8 * k + 8] = x
                tile[v, 56 - 8 * k : 64 - 8 * k] = swap_rows(x)
            for p in range(2):
                for h in range(2):
                    exits[n, p, v, :, 128 * h : 128 * h + 128] = tile[v, pl.ds(4 * h + p, 8, stride=8), :]

        @pl.when(n == me)
        def _():
            for p in range(2):
                exit_local(n, p).start()

        @pl.when(same_line(n) & (n != me))
        def _():
            for p in range(2):
                exit_copy(n, p, me).start()

        @pl.when(other_lines(n))
        def _():
            exit_copy(n, part, me).start()

    stages = stations // STEP

    def stage(t, carry):
        slot = lax.rem(t, 2)
        other = 1 - slot
        wait_recv(halo(slot))
        for n in range(REACH):
            base = HERE - 8 * (n + 1)
            pairs = [
                halo_pairs(
                    lambda k: got[slot, n, 0, k * nvar + v], lambda k: got[slot, n, 1, k * nvar + v]
                )
                for v in range(nvar)
            ]
            for j in range(8):
                keep(0, base + j, [pairs[v][j] for v in range(nvar)])
        stations_ = [station(STEP * t + i) for i in range(STEP)]
        for level in range(LEVELS):
            todo = list(range(level + 1, PAIRS))
            chunks = [todo[a : a + 2] for a in range(len(todo) % 2, len(todo), 2)]
            if len(todo) % 2:
                chunks = [todo[:1]] + chunks
            for chunk in chunks[::-1]:
                task(level, chunk, stations_)

        @pl.when(t < stages - 1)
        def _():
            @pl.when(t > 0)
            def _():
                wait_send(halo(other))

            for v in range(nvar):
                for k in range(OWN):
                    sent[other, k * nvar + v] = field[LEVELS, v, HERE + k]
            start(halo(other))
            for k in range(OWN):
                keep(0, HERE + k, [field[LEVELS, v, HERE + k] for v in range(nvar)])

        for i in range(STEP):
            leave(STEP * t + i, RECUR * (i + 1))
        return carry

    lax.fori_loop(0, stages, stage, 0)

    if stages > 1:
        wait_send(halo((stages - 2) % 2))
    wait_send(halo((stages - 1) % 2))

    def finish(n, carry):
        @pl.when(n == me)
        def _():
            for p in range(2):
                exit_local(n, p).wait()

        @pl.when(same_line(n) & (n != me))
        def _():
            for p in range(2):
                exit_copy(n, p, n).wait_send()
                exit_copy(n, p, n).wait_recv()

        @pl.when(other_lines(n))
        def _():
            exit_copy(n, part, n).wait_send()
            theirs = lax.rem(lax.div(n, 2), 2)
            exit_copy(n, theirs, n).wait_recv()

        return carry

    lax.fori_loop(0, streams, finish, 0)


def on_device(dims, inflow, shape, amp, coupling, omega, rec_coef, rec_order, zone, mask):
    streams, crosses, freqs, nvar, zones, stations = dims
    cols = inflow.shape[-1]
    anywhere = pl.BlockSpec(memory_space=pl.ANY)
    scalars = pl.BlockSpec(memory_space=pltpu.SMEM)
    f32 = jnp.float32
    dma = pltpu.SemaphoreType.DMA
    return pl.pallas_call(
        functools.partial(kernel, dims),
        out_shape=jax.ShapeDtypeStruct((1, 2, freqs, nvar, ROWS, cols), f32),
        in_specs=[anywhere, anywhere, anywhere, anywhere, scalars, scalars, scalars, anywhere, anywhere],
        out_specs=anywhere,
        scratch_shapes=[
            pltpu.VMEM((2, nvar, ROWS, cols), f32),
            pltpu.VMEM((nvar, ROWS, cols), f32),
            pltpu.VMEM((ROWS, cols), jnp.int32),
            pltpu.SMEM((zones, 4, nvar, nvar), f32),
            pltpu.VMEM((nvar, 64, 128), f32),
            pltpu.VMEM((streams, 2, freqs), f32),
            pltpu.VMEM((streams, 1, 1), jnp.int32),
            pltpu.VMEM((48 * nvar, 256), f32),
            pltpu.VMEM((zones, 48 * nvar, 256), jnp.bfloat16),
            pltpu.VMEM((9, 8, 128), f32),
            pltpu.VMEM((LEVELS + 1, nvar, PAIRS, 8, 128), f32),
            pltpu.VMEM((LEVELS, PAIRS + 1, 16 * nvar, 128), jnp.bfloat16),
            pltpu.VMEM((nvar, PAIRS, 8, 128), f32),
            pltpu.VMEM((PAIRS, 8, 128), f32),
            pltpu.VMEM((2, nvar * OWN, 8, 128), f32),
            pltpu.VMEM((2, REACH, 2, nvar * OWN, 8, 128), f32),
            pltpu.VMEM(((nvar + 1) * OWN, 8, 128), f32),
            pltpu.VMEM((REACH, 2, (nvar + 1) * OWN, 8, 128), f32),
            pltpu.VMEM((streams, 2, nvar, ROWS, cols), f32),
            dma((6,)),
            dma((2, streams)),
            dma((2, streams)),
            dma((2, REACH, 2)),
            dma((2, REACH, 2)),
            dma((REACH, 2)),
            dma((REACH, 2)),
            dma((streams, 2)),
            dma((streams, 2)),
            dma((2,)),
        ],
        compiler_params=pltpu.CompilerParams(collective_id=0, has_side_effects=True),
        name="march",
    )(inflow, shape, amp, coupling, omega, rec_coef, rec_order, zone.reshape(1, 1), mask)


def solution(mesh):
    placed = (
        P(None, None, None, "cross", None),
        P(None, "cross", None),
        P("stream", None, None),
        P(),
        P(),
        P(),
        P(),
        P("stream"),
        P("cross", None),
    )

    def whole(inflow, source_shape, source_amp, coupling, omega, rec_coef, rec_order, station_zone, solid_mask):
        streams = mesh.shape["stream"]
        crosses = mesh.shape["cross"]
        dims = (
            streams,
            crosses,
            inflow.shape[1],
            inflow.shape[2],
            coupling.shape[0],
            station_zone.shape[0],
        )
        return jax.shard_map(
            functools.partial(on_device, dims),
            mesh=mesh,
            in_specs=placed,
            out_specs=P("stream", None, None, None, "cross", None),
            check_vma=False,
        )(inflow, source_shape, source_amp, coupling, omega, rec_coef, rec_order, station_zone, solid_mask)

    return whole
```

time: 72.4 us -> 69.4 us (0.959)
  the two profiles are of different devices: /device:TPU:255 before, /device:TPU:95 now
where the time goes in v2:
time: 69.4 us; the launch traced here: 69 us
  Pallas kernels  65 us (94%)
  local copies, waits for them, and re-layouts  3.4 us (5%)
    pallas_call x1, Pallas kernels, on_device(): pl.pallas_call(functools.partial(kernel, dims), out_shape=jax.ShapeDtypeS...  65 us
    unnamed x2, local copies, waits for them, and re-layouts  3.4 us

profile of v2, /device:TPU:95, one launch (start us, length us, event | category | flops | bytes accessed | tf_op | source)
XLA Modules:
  0.0 69.0 jit_solution(14426273128278695144)
XLA Ops:
  0.7 1.4 %copy.10.coupling_in = f32[4,4,5,5]{3,2,1,0:T(8,128)} copy(f32[4,4,5,5]{3,1,2,0:T(4,128)} %param.12) | data formatting | bytes 3200 | tf_op args[3]
  2.1 65.0 %march.1 = f32[1,2,8,5,8,256]{5,4,3,2,1,0:T(8,128)} custom-call(f32[2,8,5,8,256]{4,3,2,1,0:T(8,128)} %inflow.1, f32[5,8,256]{2,1,0:T(8,128)} %shape.1, f32[1,2,8]{2,1,0:T(2,128)} %amp.1, f32[4,4,5,5]{3,2,1,0:T(8,128)} %copy.10.coupling_in, f32[8]{0:T(128)} %omega.1, f32[4]{0:T(128)} %rec_coef.1, s32[4]{0:T(128)} %rec_order.1, s32[1,1]{1,0:T(1,128)} %bitcast.1.zone, ...), custom_call_target="tpu_custom_call" | custom-call | tf_op jit(solution)/shard_map/march/pallas_call | solution.py:533
  67.1 2.0 %copy.13 = f32[1,2,8,5,8,256]{5,4,3,2,1,0:T(8,128)} copy(f32[1,2,8,5,8,256]{5,4,3,2,1,0:T(8,128)} %march.1) | data formatting | bytes 1310720

commit v3 on v2

--- a/solution.py
+++ b/solution.py
@@ -156,15 +156,15 @@
         table = {}
         for i in range(nvar):
             for w in range(i, nvar):
-                rows_iw = full(0.25 * (coupling[z, 0, i, w] + coupling[z, 0, w, i])) * side
-                cols_iw = 0.25 * (coupling[z, 1, i, w] + coupling[z, 1, w, i])
-                dot = coupling[z, 3, i, 0] * coupling[z, 3, w, 0]
+                rows_iw = full(0.25 * (coupling[z, i, 0, w] + coupling[z, w, 0, i])) * side
+                cols_iw = 0.25 * (coupling[z, i, 1, w] + coupling[z, w, 1, i])
+                dot = coupling[z, i, 3, 0] * coupling[z, w, 3, 0]
                 for k in range(1, nvar):
-                    dot = dot + coupling[z, 3, i, k] * coupling[z, 3, w, k]
+                    dot = dot + coupling[z, i, 3, k] * coupling[z, w, 3, k]
                 if i == w:
                     dot = dot + 1.0
                 visc = viscosity * dot
-                turn = 0.5 * (coupling[z, 2, i, w] - coupling[z, 2, w, i])
+                turn = 0.5 * (coupling[z, i, 2, w] - coupling[z, w, 2, i])
                 around = (visc + rows_iw, visc - rows_iw, full(visc + cols_iw), full(visc - cols_iw))
                 table[i, w] = (full(turn - 4.0 * visc),) + around
                 table[w, i] = (full(-turn - 4.0 * visc),) + around
@@ -244,18 +244,20 @@
         keep(0, HERE + k, [own[v][k] for v in range(nvar)])
         for v in range(nvar):
             sent[0, k * nvar + v] = own[v][k]
-    for v in range(nvar):
-        own = pairs_of(v, lambda p, h: shape_in[v, :, 128 * h : 128 * h + 128])
-        for k in range(OWN):
-            frame_src[v, HERE + k] = own[k]
-            sent_fix[v * OWN + k] = own[k]
-    own = pairs_of(
-        0,
-        lambda p, h: penalty * mask_in[:, 128 * h : 128 * h + 128].astype(jnp.float32) + damping,
-    )
+    fixes = [
+        pairs_of(
+            0,
+            lambda p, h: penalty * mask_in[:, 128 * h : 128 * h + 128].astype(jnp.float32) + damping,
+        )
+    ] + [
+        pairs_of(v, lambda p, h: shape_in[v, :, 128 * h : 128 * h + 128]) for v in range(nvar)
+    ]
     for k in range(OWN):
-        frame_damp[HERE + k] = own[k]
-        sent_fix[nvar * OWN + k] = own[k]
+        frame_damp[HERE + k] = fixes[0][k]
+        for v in range(nvar):
+            frame_src[v, HERE + k] = fixes[1 + v][k]
+        for m in range((nvar + 1) // 2):
+            sent_fix[m * OWN + k] = jnp.where(real, fixes[2 * m][k], fixes[2 * m + 1][k])
 
     near = [x.astype(jnp.int32) for x in above + below]
     pl.semaphore_wait(barrier, streams - 1 + functools.reduce(lambda x, y: x + y, near))
@@ -321,8 +323,8 @@
             def _():
                 copies[n][1].wait_send()
 
-    def wait_recv(copies):
-        for n in range(REACH):
+    def wait_recv(copies, blocks=range(REACH)):
+        for n in blocks:
 
             @pl.when(above[n])
             def _():
@@ -344,15 +346,19 @@
     wait_recv(fixed)
     for n in range(REACH):
         base = HERE - 8 * (n + 1)
-        for v in range(nvar + 1):
+        for m in range((nvar + 1) // 2):
             pairs = halo_pairs(
-                lambda k: got_fix[n, 0, v * OWN + k], lambda k: got_fix[n, 1, v * OWN + k]
+                lambda k: got_fix[n, 0, m * OWN + k], lambda k: got_fix[n, 1, m * OWN + k]
             )
             for j in range(8):
-                if v < nvar:
-                    frame_src[v, base + j] = pairs[j]
+                swapped = swap_parts(pairs[j])
+                one = jnp.where(real, pairs[j], swapped)
+                two = jnp.where(real, swapped, pairs[j])
+                if m:
+                    frame_src[2 * m - 1, base + j] = one
                 else:
-                    frame_damp[base + j] = pairs[j]
+                    frame_damp[base + j] = one
+                frame_src[2 * m, base + j] = two
 
     inside = {
         HERE - 1 - 8 * n: jnp.where(top, near[n].astype(jnp.float32), near[REACH + n].astype(jnp.float32))
@@ -457,6 +463,31 @@
     def stage(t, carry):
         slot = lax.rem(t, 2)
         other = 1 - slot
+        stations_ = [station(STEP * t + i) for i in range(STEP)]
+        done = [set() for _ in range(LEVELS + 1)]
+        done[0] = set(range(HERE, PAIRS))
+        own = set(range(HERE, PAIRS))
+        left = set()
+
+        def advance():
+            for level in range(LEVELS):
+                have = done[level] | {PAIRS}
+                todo = [
+                    j
+                    for j in range(level + 1, PAIRS)
+                    if {j - 1, j, j + 1} <= have and j not in done[level + 1]
+                ]
+                chunks = [todo[a : a + 2] for a in range(len(todo) % 2, len(todo), 2)]
+                if len(todo) % 2:
+                    chunks = [todo[:1]] + chunks
+                for chunk in chunks[::-1]:
+                    task(level, chunk, stations_)
+                done[level + 1].update(todo)
+                i = level // RECUR
+                if (level + 1) % RECUR == 0 and own <= done[level + 1] and i not in left and i < STEP - 1:
+                    left.add(i)
+                    leave(STEP * t + i, level + 1)
+
         wait_recv(halo(slot))
         for n in range(REACH):
             base = HERE - 8 * (n + 1)
@@ -468,14 +499,8 @@
             ]
             for j in range(8):
                 keep(0, base + j, [pairs[v][j] for v in range(nvar)])
-        stations_ = [station(STEP * t + i) for i in range(STEP)]
-        for level in range(LEVELS):
-            todo = list(range(level + 1, PAIRS))
-            chunks = [todo[a : a + 2] for a in range(len(todo) % 2, len(todo), 2)]
-            if len(todo) % 2:
-                chunks = [todo[:1]] + chunks
-            for chunk in chunks[::-1]:
-                task(level, chunk, stations_)
+            done[0].update(range(base, base + 8))
+        advance()
 
         @pl.when(t < stages - 1)
         def _():
@@ -490,8 +515,7 @@
             for k in range(OWN):
                 keep(0, HERE + k, [field[LEVELS, v, HERE + k] for v in range(nvar)])
 
-        for i in range(STEP):
-            leave(STEP * t + i, RECUR * (i + 1))
+        leave(STEP * t + STEP - 1, LEVELS)
         return carry
 
     lax.fori_loop(0, stages, stage, 0)
@@ -539,7 +563,7 @@
             pltpu.VMEM((2, nvar, ROWS, cols), f32),
             pltpu.VMEM((nvar, ROWS, cols), f32),
             pltpu.VMEM((ROWS, cols), jnp.int32),
-            pltpu.SMEM((zones, 4, nvar, nvar), f32),
+            pltpu.SMEM((zones, nvar, 4, nvar), f32),
             pltpu.VMEM((nvar, 64, 128), f32),
             pltpu.VMEM((streams, 2, freqs), f32),
             pltpu.VMEM((streams, 1, 1), jnp.int32),
@@ -552,8 +576,8 @@
             pltpu.VMEM((PAIRS, 8, 128), f32),
             pltpu.VMEM((2, nvar * OWN, 8, 128), f32),
             pltpu.VMEM((2, REACH, 2, nvar * OWN, 8, 128), f32),
-            pltpu.VMEM(((nvar + 1) * OWN, 8, 128), f32),
-            pltpu.VMEM((REACH, 2, (nvar + 1) * OWN, 8, 128), f32),
+            pltpu.VMEM(((nvar + 1) // 2 * OWN, 8, 128), f32),
+            pltpu.VMEM((REACH, 2, (nvar + 1) // 2 * OWN, 8, 128), f32),
             pltpu.VMEM((streams, 2, nvar, ROWS, cols), f32),
             dma((6,)),
             dma((2, streams)),
@@ -568,7 +592,7 @@
         ],
         compiler_params=pltpu.CompilerParams(collective_id=0, has_side_effects=True),
         name="march",
-    )(inflow, shape, amp, coupling, omega, rec_coef, rec_order, zone.reshape(1, 1), mask)
+    )(inflow, shape, amp, coupling.transpose(0, 2, 1, 3), omega, rec_coef, rec_order, zone.reshape(1, 1), mask)
 
 
 def solution(mesh):

time: 69.4 us -> 63.9 us (0.921)
  the two profiles are of different devices: /device:TPU:95 before, /device:TPU:126 now
where the time goes in v3:
time: 63.9 us; the launch traced here: 63.6 us
  Pallas kernels  61 us (95%)
  local copies, waits for them, and re-layouts  1.98 us (3%)
  between operations  0.66 us (1%)
    pallas_call x1, Pallas kernels, on_device(): pl.pallas_call(functools.partial(kernel, dims), out_shape=jax.ShapeDtypeS...  61 us
    unnamed x1, local copies, waits for them, and re-layouts  1.98 us

profile of v3, /device:TPU:126, one launch (start us, length us, event | category | flops | bytes accessed | tf_op | source)
XLA Modules:
  0.0 63.6 jit_solution(8387747961192272003)
XLA Ops:
  0.7 61.0 %march.1 = f32[1,2,8,5,8,256]{5,4,3,2,1,0:T(8,128)} custom-call(f32[2,8,5,8,256]{4,3,2,1,0:T(8,128)} %inflow.1, f32[5,8,256]{2,1,0:T(8,128)} %shape.1, f32[1,2,8]{2,1,0:T(2,128)} %amp.1, f32[4,5,4,5]{3,2,1,0:T(4,128)} %bitcast.3, f32[8]{0:T(128)} %omega.1, f32[4]{0:T(128)} %rec_coef.1, s32[4]{0:T(128)} %rec_order.1, s32[1,1]{1,0:T(1,128)} %bitcast.2.zone, ...), custom_call_target="tpu_custom_call" | custom-call | tf_op jit(solution)/shard_map/march/pallas_call | solution.py:557
  61.7 2.0 %copy.12 = f32[1,2,8,5,8,256]{5,4,3,2,1,0:T(8,128)} copy(f32[1,2,8,5,8,256]{5,4,3,2,1,0:T(8,128)} %march.1) | data formatting | bytes 1310720

commit v4 on v3

--- a/solution.py
+++ b/solution.py
@@ -95,9 +95,6 @@
         pltpu.make_async_copy(zone, zone_all.at[me], in_sem.at[4]),
         pltpu.make_async_copy(coupling_in, coupling, in_sem.at[5]),
     ]
-    for load in loads:
-        load.start()
-
     barrier = pltpu.get_barrier_semaphore()
 
     def greet(k, carry):
@@ -121,6 +118,9 @@
 
     lax.fori_loop(1, streams, greet, 0)
 
+    for load in loads:
+        load.start()
+
     for n in range(REACH):
         for missing, at in ((~above[n], 0), (~below[n], 1)):
 
@@ -130,12 +130,154 @@
                     got[slot, n, at] = jnp.zeros_like(got[slot, n, at])
                 got_fix[n, at] = jnp.zeros_like(got_fix[n, at])
 
+    def halves(x, y=None):
+        both = x if y is None else jnp.concatenate([x, y], axis=0)
+        high = both.astype(jnp.bfloat16)
+        wide = high.astype(jnp.float32)
+        low = both - wide
+        if y is None:
+            return jnp.concatenate([wide, low], axis=0).astype(jnp.bfloat16)
+        return high, low.astype(jnp.bfloat16)
+
+    def pack(level, j, at, xs):
+        at = 16 * nvar * at
+        for v in range(0, nvar - 1, 2):
+            high, low = halves(xs[v], xs[v + 1])
+            packed[level, j, at + 16 * v : at + 16 * v + 16] = high
+            packed[level, j, at + 16 * v + 16 : at + 16 * v + 32] = low
+        packed[level, j, at + 16 * nvar - 16 : at + 16 * nvar] = halves(xs[nvar - 1])
+
+    def keep(level, j, xs):
+        for v in range(nvar):
+            field[level, v, j] = xs[v]
+        if level < LEVELS:
+            pack(level, j, 0, xs)
+            if j > level:
+                across = [pltpu.roll(x, 4, 0) for x in xs]
+                east = [pltpu.roll(jnp.where(first, o, x), 127, 1) for o, x in zip(across, xs)]
+                west = [pltpu.roll(jnp.where(last, o, x), 1, 1) for o, x in zip(across, xs)]
+                pack(level, j, 1, east)
+                pack(level, j, 2, west)
+            if j == PAIRS - 1:
+                pack(level, PAIRS, 0, [swap_rows(x) for x in xs])
+
+    def pairs_of(slot, get):
+        for p in range(2):
+            for h in range(2):
+                tile[slot, pl.ds(4 * h + p, 8, stride=8), :] = get(p, h)
+        return [
+            jnp.where(top, tile[slot, 8 * k : 8 * k + 8], swap_rows(tile[slot, 56 - 8 * k : 64 - 8 * k]))
+            for k in range(OWN)
+        ]
+
+    for load in loads[:5]:
+        load.wait()
+    own = [
+        pairs_of(v, lambda p, h: nat_in[p, v, :, 128 * h : 128 * h + 128]) for v in range(nvar)
+    ]
+    for k in range(OWN):
+        keep(0, HERE + k, [own[v][k] for v in range(nvar)])
+        for v in range(nvar):
+            sent[0, k * nvar + v] = own[v][k]
+    fixes = [
+        pairs_of(
+            0,
+            lambda p, h: penalty * mask_in[:, 128 * h : 128 * h + 128].astype(jnp.float32) + damping,
+        )
+    ] + [
+        pairs_of(v, lambda p, h: shape_in[v, :, 128 * h : 128 * h + 128]) for v in range(nvar)
+    ]
+    for k in range(OWN):
+        frame_damp[HERE + k] = fixes[0][k]
+        for v in range(nvar):
+            frame_src[v, HERE + k] = fixes[1 + v][k]
+        for m in range((nvar + 1) // 2):
+            sent_fix[m * OWN + k] = jnp.where(real, fixes[2 * m][k], fixes[2 * m + 1][k])
+
+    near = [x.astype(jnp.int32) for x in above + below]
+    pl.semaphore_wait(barrier, streams - 1 + functools.reduce(lambda x, y: x + y, near))
+
+    def gather_copies(k):
+        peer = lax.rem(me + k, streams)
+        return (
+            pltpu.make_async_remote_copy(
+                zone, zone_all.at[me], gather_send.at[0, k], gather_recv.at[0, k],
+                device_id=(peer, row), device_id_type=MESH,
+            ),
+            pltpu.make_async_remote_copy(
+                amp.at[0], amp_all.at[me], gather_send.at[1, k], gather_recv.at[1, k],
+                device_id=(peer, row), device_id_type=MESH,
+            ),
+        )
+
+    def gather_start(k, carry):
+        for copy in gather_copies(k):
+            copy.start()
+        return carry
+
+
+    def both_ways(source, target, send_sems, recv_sems, n):
+        up = pltpu.make_async_remote_copy(
+            source, target.at[n, 1], send_sems.at[n, 0], recv_sems.at[n, 1],
+            device_id=(me, row - 1 - n), device_id_type=MESH,
+        )
+        down = pltpu.make_async_remote_copy(
+            source, target.at[n, 0], send_sems.at[n, 1], recv_sems.at[n, 0],
+            device_id=(me, row + 1 + n), device_id_type=MESH,
+        )
+        return up, down
+
+    def halo(slot):
+        return [
+            both_ways(sent.at[slot], got.at[slot], halo_send.at[slot], halo_recv.at[slot], n)
+            for n in range(REACH)
+        ]
+
+    fixed = [both_ways(sent_fix, got_fix, fix_send, fix_recv, n) for n in range(REACH)]
+
+    def start(copies):
+        for n in range(REACH):
+
+            @pl.when(above[n])
+            def _():
+                copies[n][0].start()
+
+            @pl.when(below[n])
+            def _():
+                copies[n][1].start()
+
+    def wait_send(copies):
+        for n in range(REACH):
+
+            @pl.when(above[n])
+            def _():
+                copies[n][0].wait_send()
+
+            @pl.when(below[n])
+            def _():
+                copies[n][1].wait_send()
+
+    def wait_recv(copies, blocks=range(REACH)):
+        for n in blocks:
+
+            @pl.when(above[n])
+            def _():
+                copies[n][1].wait_recv()
+
+            @pl.when(below[n])
+            def _():
+                copies[n][0].wait_recv()
+
+    start(fixed)
+    start(halo(0))
+    lax.fori_loop(1, streams, gather_start, 0)
+
     side = jnp.where(top, 1.0, -1.0).astype(jnp.float32)
     same = (lane & 7) == sub
     spots = {}
-    for kind in range(3):
+    for kind in range(5):
         for w in range(nvar):
-            for t in range(2):
+            for t in range(4):
                 eights = [
                     10 * kind + g - 16 * t
                     for g in range(10)
@@ -165,22 +307,19 @@
                     dot = dot + 1.0
                 visc = viscosity * dot
                 turn = 0.5 * (coupling[z, i, 2, w] - coupling[z, w, 2, i])
-                around = (visc + rows_iw, visc - rows_iw, full(visc + cols_iw), full(visc - cols_iw))
+                around = (full(visc + cols_iw), full(visc - cols_iw), visc + rows_iw, visc - rows_iw)
                 table[i, w] = (full(turn - 4.0 * visc),) + around
                 table[w, i] = (full(-turn - 4.0 * visc),) + around
         for i in range(nvar):
-            for block, kinds in ((0, (0, 1, 2)), (1, (3,)), (2, (4,))):
-                for t in range(2):
-                    value = jnp.zeros((8, 128), jnp.float32)
-                    for place, kind in enumerate(kinds):
-                        for w in range(nvar):
-                            if (place, w, t) in spots:
-                                value = jnp.where(spots[place, w, t], table[i, w][kind], value)
-                    high = value.astype(jnp.bfloat16).astype(jnp.float32)
-                    at = 8 * (2 * nvar * block + i)
-                    mix32[at : at + 8, 128 * t : 128 * t + 128] = high
-                    at = at + 8 * nvar
-                    mix32[at : at + 8, 128 * t : 128 * t + 128] = value - high
+            for t in range(4):
+                value = jnp.zeros((8, 128), jnp.float32)
+                for kind in range(5):
+                    for w in range(nvar):
+                        if (kind, w, t) in spots:
+                            value = jnp.where(spots[kind, w, t], table[i, w][kind], value)
+                high = value.astype(jnp.bfloat16).astype(jnp.float32)
+                mix32[8 * i : 8 * i + 8, 128 * t : 128 * t + 128] = high
+                mix32[8 * (nvar + i) : 8 * (nvar + i) + 8, 128 * t : 128 * t + 128] = value - high
         mix[z] = mix32[...].astype(jnp.bfloat16)
         return carry
 
@@ -201,141 +340,6 @@
         coef[k] = jnp.full((8, 128), re_part[k], jnp.float32)
     for k in range(4):
         coef[5 + k] = jnp.full((8, 128), im_part[k], jnp.float32) * flip
-
-    def halves(x, y=None):
-        both = x if y is None else jnp.concatenate([x, y], axis=0)
-        high = both.astype(jnp.bfloat16)
-        wide = high.astype(jnp.float32)
-        low = both - wide
-        if y is None:
-            return jnp.concatenate([wide, low], axis=0).astype(jnp.bfloat16)
-        return high, low.astype(jnp.bfloat16)
-
-    def pack(level, j, xs):
-        for v in range(0, nvar - 1, 2):
-            high, low = halves(xs[v], xs[v + 1])
-            packed[level, j, 16 * v : 16 * v + 16] = high
-            packed[level, j, 16 * v + 16 : 16 * v + 32] = low
-        packed[level, j, 16 * nvar - 16 : 16 * nvar] = halves(xs[nvar - 1])
-
-    def keep(level, j, xs):
-        for v in range(nvar):
-            field[level, v, j] = xs[v]
-        if level < LEVELS:
-            pack(level, j, xs)
-            if j == PAIRS - 1:
-                pack(level, PAIRS, [swap_rows(x) for x in xs])
-
-    def pairs_of(slot, get):
-        for p in range(2):
-            for h in range(2):
-                tile[slot, pl.ds(4 * h + p, 8, stride=8), :] = get(p, h)
-        return [
-            jnp.where(top, tile[slot, 8 * k : 8 * k + 8], swap_rows(tile[slot, 56 - 8 * k : 64 - 8 * k]))
-            for k in range(OWN)
-        ]
-
-    for load in loads[:5]:
-        load.wait()
-    own = [
-        pairs_of(v, lambda p, h: nat_in[p, v, :, 128 * h : 128 * h + 128]) for v in range(nvar)
-    ]
-    for k in range(OWN):
-        keep(0, HERE + k, [own[v][k] for v in range(nvar)])
-        for v in range(nvar):
-            sent[0, k * nvar + v] = own[v][k]
-    fixes = [
-        pairs_of(
-            0,
-            lambda p, h: penalty * mask_in[:, 128 * h : 128 * h + 128].astype(jnp.float32) + damping,
-        )
-    ] + [
-        pairs_of(v, lambda p, h: shape_in[v, :, 128 * h : 128 * h + 128]) for v in range(nvar)
-    ]
-    for k in range(OWN):
-        frame_damp[HERE + k] = fixes[0][k]
-        for v in range(nvar):
-            frame_src[v, HERE + k] = fixes[1 + v][k]
-        for m in range((nvar + 1) // 2):
-            sent_fix[m * OWN + k] = jnp.where(real, fixes[2 * m][k], fixes[2 * m + 1][k])
-
-    near = [x.astype(jnp.int32) for x in above + below]
-    pl.semaphore_wait(barrier, streams - 1 + functools.reduce(lambda x, y: x + y, near))
-
-    def gather_copies(k):
-        peer = lax.rem(me + k, streams)
-        return (
-            pltpu.make_async_remote_copy(
-                zone, zone_all.at[me], gather_send.at[0, k], gather_recv.at[0, k],
-                device_id=(peer, row), device_id_type=MESH,
-            ),
-            pltpu.make_async_remote_copy(
-                amp.at[0], amp_all.at[me], gather_send.at[1, k], gather_recv.at[1, k],
-                device_id=(peer, row), device_id_type=MESH,
-            ),
-        )
-
-    def gather_start(k, carry):
-        for copy in gather_copies(k):
-            copy.start()
-        return carry
-
-    lax.fori_loop(1, streams, gather_start, 0)
-
-    def both_ways(source, target, send_sems, recv_sems, n):
-        up = pltpu.make_async_remote_copy(
-            source, target.at[n, 1], send_sems.at[n, 0], recv_sems.at[n, 1],
-            device_id=(me, row - 1 - n), device_id_type=MESH,
-        )
-        down = pltpu.make_async_remote_copy(
-            source, target.at[n, 0], send_sems.at[n, 1], recv_sems.at[n, 0],
-            device_id=(me, row + 1 + n), device_id_type=MESH,
-        )
-        return up, down
-
-    def halo(slot):
-        return [
-            both_ways(sent.at[slot], got.at[slot], halo_send.at[slot], halo_recv.at[slot], n)
-            for n in range(REACH)
-        ]
-
-    fixed = [both_ways(sent_fix, got_fix, fix_send, fix_recv, n) for n in range(REACH)]
-
-    def start(copies):
-        for n in range(REACH):
-
-            @pl.when(above[n])
-            def _():
-                copies[n][0].start()
-
-            @pl.when(below[n])
-            def _():
-                copies[n][1].start()
-
-    def wait_send(copies):
-        for n in range(REACH):
-
-            @pl.when(above[n])
-            def _():
-                copies[n][0].wait_send()
-
-            @pl.when(below[n])
-            def _():
-                copies[n][1].wait_send()
-
-    def wait_recv(copies, blocks=range(REACH)):
-        for n in blocks:
-
-            @pl.when(above[n])
-            def _():
-                copies[n][1].wait_recv()
-
-            @pl.when(below[n])
-            def _():
-                copies[n][0].wait_recv()
-
-    start(halo(0))
-    start(fixed)
 
     def halo_pairs(before, after):
         outer = [jnp.where(top, before(k), after(k)) for k in range(OWN)]
@@ -399,7 +403,14 @@
     def task(level, chunk, stations_):
         here, weight = stations_[level // RECUR]
         operands = [
-            jnp.concatenate([packed[level, j], packed[level, j + 1], packed[level, j - 1]], axis=0)
+            jnp.concatenate(
+                [
+                    packed[level, j],
+                    packed[level, j + 1, 0 : 16 * nvar],
+                    packed[level, j - 1, 0 : 16 * nvar],
+                ],
+                axis=0,
+            )
             for j in chunk
         ]
         operand = operands[0] if len(chunk) == 1 else jnp.concatenate(operands, axis=1)
@@ -409,18 +420,11 @@
         base = level // RECUR * RECUR
         for a, j in enumerate(chunk):
 
-            def part_of(block, i):
-                at = 8 * (2 * nvar * block + i)
-                cols = slice(128 * a, 128 * a + 128)
-                return result[at : at + 8, cols] + result[at + 8 * nvar : at + 8 * nvar + 8, cols]
-
+            cols = slice(128 * a, 128 * a + 128)
             values = []
             for i in range(nvar):
-                east = part_of(1, i)
-                west = part_of(2, i)
-                east = pltpu.roll(jnp.where(first, pltpu.roll(east, 4, 0), east), 127, 1)
-                west = pltpu.roll(jnp.where(last, pltpu.roll(west, 4, 0), west), 1, 1)
-                value = part_of(0, i) - frame_damp[j] * field[level, i, j] + (east + west)
+                value = result[8 * i : 8 * i + 8, cols] + result[8 * (nvar + i) : 8 * (nvar + i) + 8, cols]
+                value = value - frame_damp[j] * field[level, i, j]
                 if j in inside:
                     value = value * inside[j]
                 if (level + 1) % RECUR == 0:
@@ -567,11 +571,11 @@
             pltpu.VMEM((nvar, 64, 128), f32),
             pltpu.VMEM((streams, 2, freqs), f32),
             pltpu.VMEM((streams, 1, 1), jnp.int32),
-            pltpu.VMEM((48 * nvar, 256), f32),
-            pltpu.VMEM((zones, 48 * nvar, 256), jnp.bfloat16),
+            pltpu.VMEM((16 * nvar, 512), f32),
+            pltpu.VMEM((zones, 16 * nvar, 512), jnp.bfloat16),
             pltpu.VMEM((9, 8, 128), f32),
             pltpu.VMEM((LEVELS + 1, nvar, PAIRS, 8, 128), f32),
-            pltpu.VMEM((LEVELS, PAIRS + 1, 16 * nvar, 128), jnp.bfloat16),
+            pltpu.VMEM((LEVELS, PAIRS + 1, 48 * nvar, 128), jnp.bfloat16),
             pltpu.VMEM((nvar, PAIRS, 8, 128), f32),
             pltpu.VMEM((PAIRS, 8, 128), f32),
             pltpu.VMEM((2, nvar * OWN, 8, 128), f32),

time: 63.9 us -> 63.7 us (level)
  no operation moved by 1% of the time
where the time goes in v4:
time: 63.7 us; the launch traced here: 63.5 us
  Pallas kernels  60.8 us (95%)
  local copies, waits for them, and re-layouts  1.98 us (3%)
  between operations  0.66 us (1%)
    pallas_call x1, Pallas kernels, on_device(): pl.pallas_call(functools.partial(kernel, dims), out_shape=jax.ShapeDtypeS...  60.8 us
    unnamed x1, local copies, waits for them, and re-layouts  1.98 us

profile of v4, /device:TPU:126, one launch (start us, length us, event | category | flops | bytes accessed | tf_op | source)
XLA Modules:
  0.0 63.5 jit_solution(8658273416556437657)
XLA Ops:
  0.7 60.8 %march.1 = f32[1,2,8,5,8,256]{5,4,3,2,1,0:T(8,128)} custom-call(f32[2,8,5,8,256]{4,3,2,1,0:T(8,128)} %inflow.1, f32[5,8,256]{2,1,0:T(8,128)} %shape.1, f32[1,2,8]{2,1,0:T(2,128)} %amp.1, f32[4,5,4,5]{3,2,1,0:T(4,128)} %bitcast.3, f32[8]{0:T(128)} %omega.1, f32[4]{0:T(128)} %rec_coef.1, s32[4]{0:T(128)} %rec_order.1, s32[1,1]{1,0:T(1,128)} %bitcast.2.zone, ...), custom_call_target="tpu_custom_call" | custom-call | tf_op jit(solution)/shard_map/march/pallas_call | solution.py:561
  61.5 2.0 %copy.12 = f32[1,2,8,5,8,256]{5,4,3,2,1,0:T(8,128)} copy(f32[1,2,8,5,8,256]{5,4,3,2,1,0:T(8,128)} %march.1) | data formatting | bytes 1310720
